TPU v7x, 128 devices: a whole 4x4x4 slice. The times are simulated.
128 devices in a mesh: own: 4 (over z), img: 32 (over x, y, core).
Axes of the slice: x: 4, y: 4, z: 4, core: 2. Of those that a mesh axis runs over, the one named last changes fastest.
Arguments:
- mask_field: bfloat16 [4096, 16384], P('own', 'img'), may hold values from -1 to 1
- target_field: bfloat16 [4096, 16384], P('own', 'img'), may hold values from 0 to 1
- occupancy: int32 [8, 32], replicated, may hold values 0 or 1
- kernels: float32 [2, 24, 32, 32], replicated, may hold values from -9 to 9
- weights: float32 [24], replicated, may hold values from 0.01 to 0.3
Outputs:
- gradient: float32 [4096, 16384], P('own', 'img')
All inputs are finite; a program needn't handle non-finite values.
Results may differ from a plain program's by a relative error of at most 0.0072.
Values may be sent and summed in bfloat16 or wider, within the bound.
No kernel may reach another device: no remote copies, remote signals or barrier semaphores. Data moves between devices by JAX's collectives and lax.ppermute only.
A program may use at most 64 MiB of HBM per device.

v0:
```python
import jax
import jax.numpy as jnp
import numpy as np
from jax import lax
from jax.experimental import pallas as pl
from jax.experimental.pallas import tpu as pltpu
from jax.sharding import PartitionSpec as P

TILE = 512
AMBIT = 64
FREQ = 32
KERNELS = 24
PAD = 640
GRID = 64

STEEP = 2.0
THRESHOLD = 1.5
GAMMA = 0.25

BF = jnp.bfloat16
F32 = jnp.float32


def _bf(x):
    return np.asarray(x, np.float32).astype(BF)


def _hi_lo(x):
    hi = _bf(x)
    return hi, _bf(np.asarray(x, np.float64) - hi.astype(np.float64))


def _build_tables():
    f = np.arange(FREQ) - FREQ // 2
    ang = 2 * np.pi * ((f[:, None] * np.arange(PAD)[None]) % PAD) / PAD
    c = _bf(np.cos(ang) / np.sqrt(PAD)).astype(np.float64)
    s = _bf(-np.sin(ang) / np.sqrt(PAD)).astype(np.float64)

    height, width = 2 * TILE, TILE
    first = {0: AMBIT + TILE, 1: AMBIT, 2: AMBIT - TILE, 3: AMBIT - 2 * TILE}

    def rows_of(table, r):
        out = np.zeros((FREQ, height))
        y = np.arange(height) + first[r]
        ok = (y >= 0) & (y < PAD)
        out[:, ok] = table[:, y[ok]]
        return out

    fwd = np.concatenate(
        [rows_of(c, 0), rows_of(c, 3), rows_of(s, 0), rows_of(s, 3)]
        + [rows_of(c, 1), rows_of(c, 2), rows_of(s, 1), rows_of(s, 2)],
        0,
    )

    def cols_of(table, shift, lo, hi):
        out = np.zeros((FREQ, hi - lo))
        x = np.arange(lo, hi) + shift
        ok = (x >= 0) & (x < PAD)
        out[:, ok] = table[:, x[ok]]
        return out

    t = {"fwd": _bf(fwd), "bwd": _bf(fwd.T)}
    ranges = {"mid": (AMBIT, 0, width), "left": (AMBIT + TILE, 0, 128), "right": (AMBIT - TILE, width - 128, width)}
    for name, (shift, lo, hi) in ranges.items():
        cc, ss = cols_of(c, shift, lo, hi), cols_of(s, shift, lo, hi)
        re = np.concatenate([cc.T, ss.T], 1)
        im = np.concatenate([-ss.T, cc.T], 1)
        both = np.concatenate([re, im], 0)
        t["f_" + name] = _bf(np.concatenate([both, both], 1))
        dre, dim = np.concatenate([cc, ss], 0), np.concatenate([-ss, cc], 0)
        t["b_" + name] = _bf(np.concatenate([np.concatenate([dre, dre], 0), np.concatenate([dim, dim], 0)], 1))

    grid = np.arange(GRID) * (PAD // GRID)
    hang = 2 * np.pi * ((grid[:, None] * f[None]) % PAD) / PAD
    hc, hs = np.cos(hang) / np.sqrt(FREQ), np.sin(hang) / np.sqrt(FREQ)
    tp = np.concatenate(
        [
            np.concatenate([hc.T, hs.T, -hs.T, hc.T], 1),
            np.concatenate([-hs.T, hc.T, -hc.T, -hs.T], 1),
        ],
        0,
    )
    hi, lo = _hi_lo(tp)
    t["tp"] = np.concatenate([hi, hi, hi, hi, lo, lo], 0)
    hi, lo = _hi_lo(np.concatenate([hc, hs], 1))
    t["te"] = np.concatenate([hi, hi, lo], 1)
    t["tx"] = hi.T.copy()
    v1 = np.block([[hc, -hs], [hs, hc]])
    v2 = np.block([[-hs, -hc], [hc, -hs]])
    v = np.concatenate([v1, v2], 0)
    t["tv"] = _bf(np.concatenate([v, v[:, FREQ:], -v[:, :FREQ]], 1))

    n = np.arange(1 - FREQ, FREQ)
    y = np.arange(TILE) + AMBIT
    w = np.cos(2 * np.pi * ((y[:, None, None] - grid[None, :, None]) * n[None, None, :] % PAD) / PAD).sum(-1) / GRID
    hi, lo = _hi_lo(w)
    t["tz"] = np.concatenate([hi.T, hi.T, hi.T, hi.T, lo.T, lo.T], 0)
    t["tw"] = np.concatenate([hi, hi, lo], 1)
    t["ty"] = np.concatenate([hi, hi, lo, lo], 1)
    t["tg"] = np.concatenate([hi.T, lo.T], 0)
    return t


TABLES = _build_tables()


def _dot(a, b):
    return jnp.dot(a, b, preferred_element_type=F32)


def _split(x):
    hi = x.astype(BF)
    return hi, (x - hi.astype(F32)).astype(BF)


def _low_lanes(shape):
    return lax.broadcasted_iota(jnp.int32, shape, len(shape) - 1) < 64


def _forward_kernel(mask_ref, fwd_ref, mid_ref, left_ref, right_ref, own_ref, a_ref, b_ref, acc):
    acc[...] = _dot(fwd_ref[...], mask_ref[...]).astype(BF)
    odd = lax.rem(lax.axis_index("img"), 2) == 1

    def project(lo, hi, table):
        re03, im03 = acc[0:64, lo:hi], acc[64:128, lo:hi]
        re12, im12 = acc[128:192, lo:hi], acc[192:256, lo:hi]
        lhs = jnp.concatenate(
            [jnp.concatenate([re03, im03], 1), jnp.concatenate([re12, im12], 1)], 0
        )
        out = _dot(lhs, table[...])
        return jnp.where(_low_lanes((64, 128)), out[:64], out[64:])

    own_ref[...] = project(0, 512, mid_ref)
    left = project(0, 128, left_ref)
    right = project(384, 512, right_ref)
    a_ref[...] = jnp.where(odd, left, right)
    b_ref[...] = jnp.where(odd, right, left)


def _image_kernel(
    x_ref, ua_ref, ub_ref, kk_ref, target_ref, occ_ref,
    tp_ref, te_ref, tx_ref, tv_ref, tz_ref, tw_ref, ty_ref, tg_ref,
    out_ref, p_hi, p_lo, fields, xs, yb,
):
    band, col = lax.axis_index("own"), lax.axis_index("img")
    even = lax.rem(band, 2) == 0
    inner = (band == 1) | (band == 2)
    ua = ua_ref[...]
    ub = jnp.where(inner, ub_ref[...], 0.0)
    from_up = jnp.where(even, ub, ua)
    from_down = jnp.where(even, ua, ub)
    low = _low_lanes((FREQ, 128))
    lane = lax.broadcasted_iota(jnp.int32, (FREQ, 128), 1)

    kk = kk_ref[...]
    for t, extra in enumerate((from_up, from_down)):
        m = x_ref[t * FREQ : (t + 1) * FREQ, :]
        m = pltpu.roll(m, 64, 1) + extra
        dup = jnp.where(low, m, pltpu.roll(m, 64, 1))
        swapped = pltpu.roll(dup, 32, 1)
        swapped = jnp.where(lane < 96, -swapped, swapped)
        m4 = jnp.where(low, dup, swapped)
        prod = kk * m4[None]
        hi, lo = _split(prod.reshape(KERNELS * FREQ, 128))
        half = _dot(jnp.concatenate([hi, lo, hi], 1), tp_ref[...])
        hi, lo = _split(half)
        p_hi[t] = hi.reshape(KERNELS, FREQ, 256)
        p_lo[t] = lo.reshape(KERNELS, FREQ, 256)

    total = jnp.zeros((GRID, 256), F32)
    for k in range(KERNELS):
        def halves(ref):
            return jnp.concatenate(
                [
                    jnp.concatenate([ref[0, k, :, :128], ref[1, k, :, :128]], 1),
                    jnp.concatenate([ref[0, k, :, 128:], ref[1, k, :, 128:]], 1),
                ],
                0,
            )
        hi = halves(p_hi)
        e = _dot(te_ref[...], jnp.concatenate([hi, halves(p_lo), hi], 0))
        fields[k] = e
        total = total + e * e

    hi, lo = _split(jnp.concatenate([total[:, :128], total[:, 128:]], 0))
    z = _dot(jnp.concatenate([hi, lo, hi], 1), tz_ref[...])
    pulls = []
    rows = 128
    for t in range(2):
        hi, lo = _split(z[t * GRID : (t + 1) * GRID])
        stack = jnp.concatenate([hi, lo, hi], 0)
        for c in range(TILE // rows):
            at = c * rows
            intensity = _dot(tw_ref[at : at + rows], stack)
            th = jnp.tanh((0.5 * STEEP) * (intensity - THRESHOLD))
            wanted = target_ref[t * TILE + at : t * TILE + at + rows, :].astype(F32)
            sens = (0.5 * STEEP) * (0.5 + 0.5 * th - wanted) * (1.0 - th * th)
            y = _dot(sens.astype(BF), ty_ref[...])
            yb[at : at + rows, :] = (y[:, :128] + y[:, 128:]).astype(BF)
        g = _dot(tg_ref[...], yb[...])
        pulls.append(2.0 * (g[:GRID] + g[GRID:]))
    pull = jnp.concatenate(pulls, 1)

    for k in range(KERNELS):
        q = (pull * fields[k]).astype(BF)
        x = _dot(tx_ref[...], q).astype(BF)
        for t in range(2):
            at = t * 128
            xs[t, k] = jnp.concatenate([x[:32, at : at + 128], x[32:, at : at + 128]], 1)

    d = _dot(xs[...].reshape(2 * KERNELS * FREQ, 256), tv_ref[...])
    d = d.reshape(2, KERNELS, FREQ, 128)
    parts = []
    for t in range(2):
        s = jnp.sum(kk * d[t], 0)
        s = s + pltpu.roll(s, 64, 1)
        parts.append(jnp.where(occ_ref[2 * band + t, col] > 0, s, 0.0))
    out_ref[...] = jnp.where(low, parts[0], parts[1])


def _backward_kernel(
    c_ref, a_ref, b_ref, mask_ref, bwd_ref, mid_ref, left_ref, right_ref, out_ref, du
):
    @pl.when(pl.program_id(0) == 0)
    def _():
        col = lax.axis_index("img")
        odd = lax.rem(col, 2) == 1
        a = a_ref[...]
        b = jnp.where((col > 0) & (col < 31), b_ref[...], 0.0)
        left = jnp.where(odd, a, b)
        right = jnp.where(odd, b, a)
        low = _low_lanes((FREQ, 128))

        def stacked(val):
            out = []
            for r, (row, first) in enumerate(((32, True), (32, False), (0, True), (0, False))):
                x = val[row : row + 32]
                other = pltpu.roll(x, 64, 1)
                dup = jnp.where(low, x, other) if first else jnp.where(low, other, x)
                hi, lo = _split(dup)
                out.append(jnp.where(low, hi.astype(F32), lo.astype(F32)).astype(BF))
            return jnp.concatenate(out, 0)

        mid = _dot(stacked(c_ref[...]), mid_ref[...])
        lo = _dot(stacked(left), left_ref[...])
        hi = _dot(stacked(right), right_ref[...])
        for part in range(2):
            m = mid[:, part * 512 : part * 512 + 512]
            m = jnp.concatenate(
                [m[:, :128] + lo[:, part * 128 : part * 128 + 128], m[:, 128:384],
                 m[:, 384:] + hi[:, part * 128 : part * 128 + 128]], 1
            ).astype(BF)
            du[part * 64 : part * 64 + 64, :] = m[:64]
            du[128 + part * 64 : 128 + part * 64 + 64, :] = m[64:]

    values = mask_ref[...].astype(F32)
    penalty = GAMMA * 4.0 * values * (values * values - 1.0)
    out_ref[...] = _dot(bwd_ref[...], du[...]) + penalty


def _permute(value, target):
    bands, cols = lax.axis_size("own"), lax.axis_size("img")
    pairs = []
    for a in range(bands):
        for b in range(cols):
            c, d = target(a, b)
            pairs.append((a * cols + b, c * cols + d))
    return lax.ppermute(value, ("own", "img"), pairs)


def _swap_even(i, n):
    return i ^ 1


def _swap_odd(i, n):
    j = ((i + 1) ^ 1) - 1
    return j if 0 <= j < n else i


def _img_even(a, b):
    return a, _swap_even(b, 32)


def _img_odd(a, b):
    return a, _swap_odd(b, 32)


def _own_even(a, b):
    return _swap_even(a, 4), b


def _own_odd(a, b):
    return _swap_odd(a, 4), b


def on_device(mask_field, target_field, occupancy, kernels, weights):
    t = {name: jnp.asarray(value) for name, value in TABLES.items()}
    band, col = lax.axis_index("own"), lax.axis_index("img")
    vmem = pl.BlockSpec(memory_space=pltpu.VMEM)
    small = jax.ShapeDtypeStruct((64, 128), F32)

    own, send_a, send_b = pl.pallas_call(
        _forward_kernel,
        out_shape=[small] * 3,
        in_specs=[vmem] * 5,
        out_specs=[vmem] * 3,
        scratch_shapes=[pltpu.VMEM((256, 512), BF)],
        name="forward",
    )(mask_field, t["fwd"], t["f_mid"], t["f_left"], t["f_right"])

    wide = jnp.sqrt(weights)[:, None, None] * kernels
    kk = jnp.concatenate([wide[0], wide[0], wide[1], wide[1]], -1)

    got_a = _permute(send_a, _img_even)
    got_b = _permute(send_b, _img_odd)
    x1 = own + got_a + jnp.where((col > 0) & (col < 31), got_b, 0.0)
    even = lax.rem(band, 2) == 0
    ua = _permute(jnp.where(even, x1[32:], x1[:32]), _own_even)
    ub = _permute(jnp.where(even, x1[:32], x1[32:]), _own_odd)

    grads = pl.pallas_call(
        _image_kernel,
        out_shape=jax.ShapeDtypeStruct((FREQ, 128), F32),
        in_specs=[vmem] * 5 + [pl.BlockSpec(memory_space=pltpu.SMEM)] + [vmem] * 8,
        out_specs=vmem,
        scratch_shapes=[
            pltpu.VMEM((2, KERNELS, FREQ, 256), BF),
            pltpu.VMEM((2, KERNELS, FREQ, 256), BF),
            pltpu.VMEM((KERNELS, GRID, 256), F32),
            pltpu.VMEM((2, KERNELS, FREQ, 256), BF),
            pltpu.VMEM((TILE, 128), BF),
        ],
        name="image",
    )(
        x1, ua, ub, kk, target_field, occupancy,
        t["tp"], t["te"], t["tx"], t["tv"], t["tz"], t["tw"], t["ty"], t["tg"],
    )

    da = _permute(grads, _own_even)
    db = _permute(grads, _own_odd)
    inner = (band == 1) | (band == 2)
    db = jnp.where(inner, db, 0.0)
    above = jnp.where(even, db, da)
    below = jnp.where(even, da, db)
    center = jnp.concatenate([grads, jnp.concatenate([above[:, 64:], below[:, :64]], 1)], 0)
    side_a = _permute(center, _img_even)
    side_b = _permute(center, _img_odd)

    rows = 256
    whole = lambda shape: pl.BlockSpec(shape, lambda i: (0, 0))
    return pl.pallas_call(
        _backward_kernel,
        grid=(2 * TILE // rows,),
        out_shape=jax.ShapeDtypeStruct((2 * TILE, TILE), F32),
        in_specs=[whole((64, 128))] * 3
        + [
            pl.BlockSpec((rows, TILE), lambda i: (i, 0)),
            pl.BlockSpec((rows, 256), lambda i: (i, 0)),
            whole((128, 1024)),
            whole((128, 256)),
            whole((128, 256)),
        ],
        out_specs=pl.BlockSpec((rows, TILE), lambda i: (i, 0)),
        scratch_shapes=[pltpu.VMEM((256, TILE), BF)],
        name="backward",
    )(center, side_a, side_b, mask_field, t["bwd"], t["b_mid"], t["b_left"], t["b_right"])


def solution(mesh):
    return jax.shard_map(
        on_device,
        mesh=mesh,
        in_specs=(P("own", "img"), P("own", "img"), P(), P(), P()),
        out_specs=P("own", "img"),
        check_vma=False,
    )
```

profile of v0, /device:TPU:36, one launch (start us, length us, event | category | flops | bytes accessed | tf_op | source)
XLA Modules:
  0.0 45.3 jit_solution(7702099513587594770)
XLA Ops:
  0.0 2.8 %forward.1 = (f32[64,128]{1,0:T(8,128)}, f32[64,128]{1,0:T(8,128)}, f32[64,128]{1,0:T(8,128)}) custom-call(bf16[1024,512]{1,0:T(8,128)(2,1)} %mask_ref.3, bf16[256,1024]{1,0:T(8,128)(2,1)} %constant.53.clone.fwd_ref, bf16[1024,128]{1,0:T(8,128)(2,1)} %constant.55.clone.mid_ref, bf16[256,128]{1,0:T(8,128)(2,1)} %constant.57.clone.left_ref, ...), custom_call_target="tpu_custom_call" | custom-call | tf_op jit(solution)/shard_map/forward/pallas_call | solution.py:302
  2.8 5.0 %collective-permute-start.1 = (f32[64,128]{1,0:T(8,128)}, f32[64,128]{1,0:T(8,128)S(1)}, u32[]{:S(2)}, u32[]{:S(2)}) collective-permute-start(f32[64,128]{1,0:T(8,128)} %get-tuple-element.10), channel_id=1, source_target_pairs={{0,0},{1,2},{2,1},{3,4},{4,3},{5,6},{6,5},{7,8},{8,7},{9,10},{10,9... | collective-permute-start | bytes 98312 | tf_op jit(solution)/shard_map/ppermute | solution.py:268
  7.8 0.7 %sqrt.3 = f32[24]{0:T(128)S(1)} sqrt(f32[24]{0:T(128)} %param.25) | non-fusion elementwise | bytes 192 | tf_op jit(solution)/shard_map/sqrt | solution.py:311
  8.4 0.1 broadcast_multiply_fusion
  8.7 1.8 %collective-permute-done.1 = f32[64,128]{1,0:T(8,128)S(1)} collective-permute-done((f32[64,128]{1,0:T(8,128)}, f32[64,128]{1,0:T(8,128)S(1)}, u32[]{:S(2)}, u32[]{:S(2)}) %collective-permute-start.1) | collective-permute-done | bytes 32800 | tf_op jit(solution)/shard_map/ppermute | solution.py:268
  10.5 3.8 %collective-permute-start.3 = (f32[32,128]{1,0:T(8,128)S(1)}, f32[32,128]{1,0:T(8,128)S(1)}, u32[]{:S(2)}, u32[]{:S(2)}) collective-permute-start(f32[32,128]{1,0:T(8,128)S(1)} %get-tuple-element.15), channel_id=1, source_target_pairs={{0,0},{1,1},{2,2},{3,3},{4,4},{5,5},{6,6},{7,7},{8,8},{9,9},{10,10... | collective-permute-start | bytes 49160 | tf_op jit(solution)/shard_map/ppermute | solution.py:268
  14.3 0.1 collective-permute-start.2
  14.4 1.1 %pad_maximum_fusion.kk_ref = f32[24,32,128]{2,1,0:T(8,128)} fusion(f32[24,32,32]{2,1,0:T(8,128)S(1)} %get-tuple-element.12, f32[24,32,32]{2,1,0:T(8,128)S(1)} %get-tuple-element.11), kind=kLoop, calls=%fused_computation.2 | loop fusion | flops 294912 | bytes 589824 | tf_op jit(solution)/shard_map/concatenate | solution.py:312
  15.5 0.6 %collective-permute-done.3.ub_ref = f32[32,128]{1,0:T(8,128)S(1)} collective-permute-done((f32[32,128]{1,0:T(8,128)S(1)}, f32[32,128]{1,0:T(8,128)S(1)}, u32[]{:S(2)}, u32[]{:S(2)}) %collective-permute-start.3) | collective-permute-done | bytes 16416 | tf_op jit(solution)/shard_map/ppermute | solution.py:268
  16.1 2.0 %collective-permute-done.2.ua_ref = f32[32,128]{1,0:T(8,128)S(1)} collective-permute-done((f32[32,128]{1,0:T(8,128)S(1)}, f32[32,128]{1,0:T(8,128)S(1)}, u32[]{:S(2)}, u32[]{:S(2)}) %collective-permute-start.2) | collective-permute-done | bytes 16416 | tf_op jit(solution)/shard_map/ppermute | solution.py:268
  18.2 0.6 %copy-done.7 = f32[32,128]{1,0:T(8,128)} copy-done((f32[32,128]{1,0:T(8,128)}, f32[32,128]{1,0:T(8,128)S(1)}, u32[]{:S(2)}) %copy-start.7) | copy-done | bytes 16408
  18.8 6.2 %image.1 = f32[32,128]{1,0:T(8,128)} custom-call(f32[64,128]{1,0:T(8,128)} %copy-done.1, f32[32,128]{1,0:T(8,128)} %copy-done.7, f32[32,128]{1,0:T(8,128)} %copy-done.6, f32[24,32,128]{2,1,0:T(8,128)} %pad_maximum_fusion.kk_ref, bf16[1024,512]{1,0:T(8,128)(2,1)} %target_ref.1, s32[8,32]{1,0:T(8,128)} %occ_ref.1, bf16[384,256]{1,0:T(8,128)(2,1)} %constant.61.clone.tp_ref, ...), custom_call_target="tpu_custom_call" | custom-call | tf_op jit(solution)/shard_map/image/pallas_call | solution.py:321
  24.9 2.4 %collective-permute-start.4 = (f32[32,128]{1,0:T(8,128)}, f32[32,128]{1,0:T(8,128)S(1)}, u32[]{:S(2)}, u32[]{:S(2)}) collective-permute-start(f32[32,128]{1,0:T(8,128)} %image.1), channel_id=1, source_target_pairs={{0,0},{1,1},{2,2},{3,3},{4,4},{5,5},{6,6},{7,7},{8,8},{9,9},{10,10... | collective-permute-start | bytes 49160 | tf_op jit(solution)/shard_map/ppermute | solution.py:268
  27.3 0.1 collective-permute-start.5
  27.4 3.3 %collective-permute-done.4 = f32[32,128]{1,0:T(8,128)S(1)} collective-permute-done((f32[32,128]{1,0:T(8,128)}, f32[32,128]{1,0:T(8,128)S(1)}, u32[]{:S(2)}, u32[]{:S(2)}) %collective-permute-start.4) | collective-permute-done | bytes 16416 | tf_op jit(solution)/shard_map/ppermute | solution.py:268
  30.8 0.6 %collective-permute-done.5 = f32[32,128]{1,0:T(8,128)S(1)} collective-permute-done((f32[32,128]{1,0:T(8,128)}, f32[32,128]{1,0:T(8,128)S(1)}, u32[]{:S(2)}, u32[]{:S(2)}) %collective-permute-start.5) | collective-permute-done | bytes 16416 | tf_op jit(solution)/shard_map/ppermute | solution.py:268
  31.4 0.1 slice_select_fusion.1
  31.4 0.8 %maximum_maximum_fusion.c_ref = f32[64,128]{1,0:T(8,128)S(1)} fusion(f32[32,64]{1,0:T(8,128)S(1)} %get-tuple-element.14, f32[32,64]{1,0:T(8,128)S(1)} %get-tuple-element.13, f32[32,128]{1,0:T(8,128)} %image.1), kind=kLoop, calls=%fused_computation.4 | loop fusion | flops 16384 | bytes 65536 | tf_op jit(solution)/shard_map/concatenate | solution.py:345
  32.2 2.6 %collective-permute-start.7 = (f32[64,128]{1,0:T(8,128)S(1)}, f32[64,128]{1,0:T(8,128)S(1)}, u32[]{:S(2)}, u32[]{:S(2)}) collective-permute-start(f32[64,128]{1,0:T(8,128)S(1)} %maximum_maximum_fusion.c_ref), channel_id=1, source_target_pairs={{0,0},{1,2},{2,1},{3,4},{4,3},{5,6},{6,5},{7,8},{8,7},{9,10},{10,9... | collective-permute-start | bytes 98312 | tf_op jit(solution)/shard_map/ppermute | solution.py:268
  34.8 0.1 collective-permute-start.6
  34.9 4.7 %collective-permute-done.7.b_ref = f32[64,128]{1,0:T(8,128)S(1)} collective-permute-done((f32[64,128]{1,0:T(8,128)S(1)}, f32[64,128]{1,0:T(8,128)S(1)}, u32[]{:S(2)}, u32[]{:S(2)}) %collective-permute-start.7) | collective-permute-done | bytes 32800 | tf_op jit(solution)/shard_map/ppermute | solution.py:268
  39.6 0.6 %copy-done.3 = f32[64,128]{1,0:T(8,128)} copy-done((f32[64,128]{1,0:T(8,128)}, f32[64,128]{1,0:T(8,128)S(1)}, u32[]{:S(2)}) %copy-start.3) | copy-done | bytes 32792
  40.2 0.6 %copy-done.4 = f32[64,128]{1,0:T(8,128)} copy-done((f32[64,128]{1,0:T(8,128)}, f32[64,128]{1,0:T(8,128)S(1)}, u32[]{:S(2)}) %copy-start.4) | copy-done | bytes 32792
  40.8 4.5 %backward.1 = f32[1024,512]{1,0:T(8,128)} custom-call(f32[64,128]{1,0:T(8,128)} %copy-done.2, f32[64,128]{1,0:T(8,128)} %copy-done.4, f32[64,128]{1,0:T(8,128)} %copy-done.3, bf16[1024,512]{1,0:T(8,128)(2,1)} %mask_ref.3, bf16[1024,256]{1,0:T(8,128)(2,1)} %constant.54.clone.bwd_ref, bf16[128,1024]{1,0:T(8,128)(2,1)} %constant.56.clone.mid_ref, ...), custom_call_target="tpu_custom_call" | custom-call | tf_op jit(solution)/shard_map/backward/pallas_call | solution.py:351
  (20 shorter events, 0.1 us)
Async XLA Ops:
  0.0 8.4 %copy-start = (f32[2,24,32,32]{3,2,1,0:T(8,128)S(1)}, f32[2,24,32,32]{3,2,1,0:T(8,128)}, u32[]{:S(2)}) copy-start(f32[2,24,32,32]{3,2,1,0:T(8,128)} %param.24) | copy-start | bytes 589828
  2.8 7.7 %copy-start.5 = (f32[64,128]{1,0:T(8,128)S(1)}, f32[64,128]{1,0:T(8,128)}, u32[]{:S(2)}) copy-start(f32[64,128]{1,0:T(8,128)} %get-tuple-element.8) | copy-start | bytes 98308
  2.8 5.9 %collective-permute-start = (f32[64,128]{1,0:T(8,128)}, f32[64,128]{1,0:T(8,128)S(1)}, u32[]{:S(2)}, u32[]{:S(2)}) collective-permute-start(f32[64,128]{1,0:T(8,128)} %get-tuple-element.9), channel_id=1, source_target_pairs={{0,1},{1,0},{2,3},{3,2},{4,5},{5,4},{6,7},{7,6},{8,9},{9,8},{10,11... | collective-permute-start | bytes 98312 | tf_op jit(solution)/shard_map/ppermute | solution.py:268
  2.8 7.7 %collective-permute-start.1 = (f32[64,128]{1,0:T(8,128)}, f32[64,128]{1,0:T(8,128)S(1)}, u32[]{:S(2)}, u32[]{:S(2)}) collective-permute-start(f32[64,128]{1,0:T(8,128)} %get-tuple-element.10), channel_id=1, source_target_pairs={{0,0},{1,2},{2,1},{3,4},{4,3},{5,6},{6,5},{7,8},{8,7},{9,10},{10,9... | collective-permute-start | bytes 98312 | tf_op jit(solution)/shard_map/ppermute | solution.py:268
  10.5 7.7 %copy-start.1 = (f32[64,128]{1,0:T(8,128)}, f32[64,128]{1,0:T(8,128)S(1)}, u32[]{:S(2)}) copy-start(f32[64,128]{1,0:T(8,128)S(1)} %select_add_fusion.x_ref) | copy-start | bytes 98308
  10.5 5.6 %collective-permute-start.3 = (f32[32,128]{1,0:T(8,128)S(1)}, f32[32,128]{1,0:T(8,128)S(1)}, u32[]{:S(2)}, u32[]{:S(2)}) collective-permute-start(f32[32,128]{1,0:T(8,128)S(1)} %get-tuple-element.15), channel_id=1, source_target_pairs={{0,0},{1,1},{2,2},{3,3},{4,4},{5,5},{6,6},{7,7},{8,8},{9,9},{10,10... | collective-permute-start | bytes 49160 | tf_op jit(solution)/shard_map/ppermute | solution.py:268
  14.3 3.8 %collective-permute-start.2 = (f32[32,128]{1,0:T(8,128)S(1)}, f32[32,128]{1,0:T(8,128)S(1)}, u32[]{:S(2)}, u32[]{:S(2)}) collective-permute-start(f32[32,128]{1,0:T(8,128)S(1)} %get-tuple-element.16), channel_id=1, source_target_pairs={{0,32},{1,33},{2,34},{3,35},{4,36},{5,37},{6,38},{7,39},{8,40},{9,... | collective-permute-start | bytes 49160 | tf_op jit(solution)/shard_map/ppermute | solution.py:268
  16.1 2.0 %copy-start.6 = (f32[32,128]{1,0:T(8,128)}, f32[32,128]{1,0:T(8,128)S(1)}, u32[]{:S(2)}) copy-start(f32[32,128]{1,0:T(8,128)S(1)} %collective-permute-done.3.ub_ref) | copy-start | bytes 49156
  18.1 0.6 %copy-start.7 = (f32[32,128]{1,0:T(8,128)}, f32[32,128]{1,0:T(8,128)S(1)}, u32[]{:S(2)}) copy-start(f32[32,128]{1,0:T(8,128)S(1)} %collective-permute-done.2.ua_ref) | copy-start | bytes 49156
  24.9 5.8 %collective-permute-start.4 = (f32[32,128]{1,0:T(8,128)}, f32[32,128]{1,0:T(8,128)S(1)}, u32[]{:S(2)}, u32[]{:S(2)}) collective-permute-start(f32[32,128]{1,0:T(8,128)} %image.1), channel_id=1, source_target_pairs={{0,0},{1,1},{2,2},{3,3},{4,4},{5,5},{6,6},{7,7},{8,8},{9,9},{10,10... | collective-permute-start | bytes 49160 | tf_op jit(solution)/shard_map/ppermute | solution.py:268
  27.3 4.0 %collective-permute-start.5 = (f32[32,128]{1,0:T(8,128)}, f32[32,128]{1,0:T(8,128)S(1)}, u32[]{:S(2)}, u32[]{:S(2)}) collective-permute-start(f32[32,128]{1,0:T(8,128)} %image.1), channel_id=1, source_target_pairs={{0,32},{1,33},{2,34},{3,35},{4,36},{5,37},{6,38},{7,39},{8,40},{9,... | collective-permute-start | bytes 49160 | tf_op jit(solution)/shard_map/ppermute | solution.py:268
  32.2 7.3 %copy-start.2 = (f32[64,128]{1,0:T(8,128)}, f32[64,128]{1,0:T(8,128)S(1)}, u32[]{:S(2)}) copy-start(f32[64,128]{1,0:T(8,128)S(1)} %maximum_maximum_fusion.c_ref) | copy-start | bytes 98308
  32.2 7.3 %collective-permute-start.7 = (f32[64,128]{1,0:T(8,128)S(1)}, f32[64,128]{1,0:T(8,128)S(1)}, u32[]{:S(2)}, u32[]{:S(2)}) collective-permute-start(f32[64,128]{1,0:T(8,128)S(1)} %maximum_maximum_fusion.c_ref), channel_id=1, source_target_pairs={{0,0},{1,2},{2,1},{3,4},{4,3},{5,6},{6,5},{7,8},{8,7},{9,10},{10,9... | collective-permute-start | bytes 98312 | tf_op jit(solution)/shard_map/ppermute | solution.py:268
  34.8 4.8 %collective-permute-start.6 = (f32[64,128]{1,0:T(8,128)S(1)}, f32[64,128]{1,0:T(8,128)S(1)}, u32[]{:S(2)}, u32[]{:S(2)}) collective-permute-start(f32[64,128]{1,0:T(8,128)S(1)} %maximum_maximum_fusion.c_ref), channel_id=1, source_target_pairs={{0,1},{1,0},{2,3},{3,2},{4,5},{5,4},{6,7},{7,6},{8,9},{9,8},{10,11... | collective-permute-start | bytes 98312 | tf_op jit(solution)/shard_map/ppermute | solution.py:268
  39.6 0.6 %copy-start.3 = (f32[64,128]{1,0:T(8,128)}, f32[64,128]{1,0:T(8,128)S(1)}, u32[]{:S(2)}) copy-start(f32[64,128]{1,0:T(8,128)S(1)} %collective-permute-done.7.b_ref) | copy-start | bytes 98308
  40.2 0.6 %copy-start.4 = (f32[64,128]{1,0:T(8,128)}, f32[64,128]{1,0:T(8,128)S(1)}, u32[]{:S(2)}) copy-start(f32[64,128]{1,0:T(8,128)S(1)} %collective-permute-done.6.a_ref) | copy-start | bytes 98308
where the time goes:
time: 45.8 us; the launch traced here: 45.3 us
  starting transfers between devices  14.1 us (31%)
  Pallas kernels  13.4 us (29%)
  waiting for transfers between devices  13 us (28%)
  local copies, waits for them, and re-layouts  2.54 us (6%)
  other arithmetic  2.13 us (5%)
    ppermute x8, starting transfers between devices, _permute(): return lax.ppermute(value, ('own', 'img'), pairs)  14.1 us
    ppermute x8, waiting for transfers between devices, _permute(): return lax.ppermute(value, ('own', 'img'), pairs)  13 us
    pallas_call x1, Pallas kernels, on_device(): pl.pallas_call(_image_kernel, out_shape=jax.ShapeDtypeStruct((FREQ, 128),...  6.16 us
    pallas_call x1, Pallas kernels, on_device(): pl.pallas_call(_backward_kernel, grid=(2 * TILE // rows,), out_shape=jax....  4.52 us
    pallas_call x1, Pallas kernels, on_device(): pl.pallas_call(_forward_kernel, out_shape=[small] * 3, in_specs=[vmem] *...  2.76 us
    unnamed x16, local copies, waits for them, and re-layouts  1.82 us
    concatenate x1, other arithmetic, on_device(): kk = jnp.concatenate([wide[0], wide[0], wide[1], wide[1]], -1)  1.12 us
  transfers between devices with their start and end apart: 8, of which 6 were waited for; matrix products, arithmetic and copies ran while one was open for 4% of the time, Pallas kernels for 0%

commit v1 on v0

--- a/solution.py
+++ b/solution.py
@@ -37,19 +37,23 @@
     s = _bf(-np.sin(ang) / np.sqrt(PAD)).astype(np.float64)
 
     height, width = 2 * TILE, TILE
-    first = {0: AMBIT + TILE, 1: AMBIT, 2: AMBIT - TILE, 3: AMBIT - 2 * TILE}
-
-    def rows_of(table, r):
-        out = np.zeros((FREQ, height))
-        y = np.arange(height) + first[r]
+
+    def rows_of(table, first, lo, hi):
+        out = np.zeros((FREQ, hi - lo))
+        y = np.arange(lo, hi) + first
         ok = (y >= 0) & (y < PAD)
         out[:, ok] = table[:, y[ok]]
         return out
 
-    fwd = np.concatenate(
-        [rows_of(c, 0), rows_of(c, 3), rows_of(s, 0), rows_of(s, 3)]
-        + [rows_of(c, 1), rows_of(c, 2), rows_of(s, 1), rows_of(s, 2)],
-        0,
+    own_rows = [
+        np.concatenate([rows_of(tb, first, 0, height), rows_of(tb, first, -AMBIT, 0), rows_of(tb, first, height, height + AMBIT)], 1)
+        for first in (AMBIT, AMBIT - TILE)
+        for tb in (c, s)
+    ]
+    fwd = np.concatenate(own_rows, 0)
+    first = {0: AMBIT + TILE, 1: AMBIT, 2: AMBIT - TILE, 3: AMBIT - 2 * TILE}
+    bwd = np.concatenate(
+        [rows_of(tb, first[r], 0, height) for pair in ((0, 3), (1, 2)) for tb in (c, s) for r in pair], 0
     )
 
     def cols_of(table, shift, lo, hi):
@@ -59,7 +63,7 @@
         out[:, ok] = table[:, x[ok]]
         return out
 
-    t = {"fwd": _bf(fwd), "bwd": _bf(fwd.T)}
+    t = {"fwd": _bf(fwd[:, :height]), "fwd_ambit": _bf(fwd[:, height:]), "bwd": _bf(bwd.T)}
     ranges = {"mid": (AMBIT, 0, width), "left": (AMBIT + TILE, 0, 128), "right": (AMBIT - TILE, width - 128, width)}
     for name, (shift, lo, hi) in ranges.items():
         cc, ss = cols_of(c, shift, lo, hi), cols_of(s, shift, lo, hi)
@@ -117,18 +121,28 @@
     return lax.broadcasted_iota(jnp.int32, shape, len(shape) - 1) < 64
 
 
-def _forward_kernel(mask_ref, fwd_ref, mid_ref, left_ref, right_ref, own_ref, a_ref, b_ref, acc):
-    acc[...] = _dot(fwd_ref[...], mask_ref[...]).astype(BF)
+def _forward_kernel(
+    mask_ref, ha_ref, hb_ref, fwd_ref, ambit_ref, mid_ref, left_ref, right_ref, own_ref, a_ref, b_ref, acc
+):
+    band = lax.axis_index("own")
+    even = lax.rem(band, 2) == 0
+    inner = (band == 1) | (band == 2)
     odd = lax.rem(lax.axis_index("img"), 2) == 1
+    ha = ha_ref[...].astype(F32)
+    hb = jnp.where(inner, hb_ref[...].astype(F32), 0.0)
+    ambit = jnp.concatenate([jnp.where(even, hb, ha), jnp.where(even, ha, hb)], 0).astype(BF)
+    acc[...] = (_dot(fwd_ref[...], mask_ref[...]) + _dot(ambit_ref[...], ambit)).astype(BF)
 
     def project(lo, hi, table):
-        re03, im03 = acc[0:64, lo:hi], acc[64:128, lo:hi]
-        re12, im12 = acc[128:192, lo:hi], acc[192:256, lo:hi]
         lhs = jnp.concatenate(
-            [jnp.concatenate([re03, im03], 1), jnp.concatenate([re12, im12], 1)], 0
+            [
+                jnp.concatenate([acc[0:32, lo:hi], acc[32:64, lo:hi]], 1),
+                jnp.concatenate([acc[64:96, lo:hi], acc[96:128, lo:hi]], 1),
+            ],
+            0,
         )
         out = _dot(lhs, table[...])
-        return jnp.where(_low_lanes((64, 128)), out[:64], out[64:])
+        return jnp.where(_low_lanes((FREQ, 128)), out[:FREQ], out[FREQ:])
 
     own_ref[...] = project(0, 512, mid_ref)
     left = project(0, 128, left_ref)
@@ -138,25 +152,19 @@
 
 
 def _image_kernel(
-    x_ref, ua_ref, ub_ref, kk_ref, target_ref, occ_ref,
+    x_ref, xa_ref, xb_ref, kk_ref, target_ref, occ_ref,
     tp_ref, te_ref, tx_ref, tv_ref, tz_ref, tw_ref, ty_ref, tg_ref,
     out_ref, p_hi, p_lo, fields, xs, yb,
 ):
     band, col = lax.axis_index("own"), lax.axis_index("img")
-    even = lax.rem(band, 2) == 0
-    inner = (band == 1) | (band == 2)
-    ua = ua_ref[...]
-    ub = jnp.where(inner, ub_ref[...], 0.0)
-    from_up = jnp.where(even, ub, ua)
-    from_down = jnp.where(even, ua, ub)
+    m = x_ref[...] + xa_ref[...] + jnp.where((col > 0) & (col < 31), xb_ref[...], 0.0)
+    turned = pltpu.roll(m, 64, 1)
     low = _low_lanes((FREQ, 128))
     lane = lax.broadcasted_iota(jnp.int32, (FREQ, 128), 1)
 
     kk = kk_ref[...]
-    for t, extra in enumerate((from_up, from_down)):
-        m = x_ref[t * FREQ : (t + 1) * FREQ, :]
-        m = pltpu.roll(m, 64, 1) + extra
-        dup = jnp.where(low, m, pltpu.roll(m, 64, 1))
+    for t in range(2):
+        dup = jnp.where(low, m, turned) if t == 0 else jnp.where(low, turned, m)
         swapped = pltpu.roll(dup, 32, 1)
         swapped = jnp.where(lane < 96, -swapped, swapped)
         m4 = jnp.where(low, dup, swapped)
@@ -218,44 +226,68 @@
     out_ref[...] = jnp.where(low, parts[0], parts[1])
 
 
-def _backward_kernel(
-    c_ref, a_ref, b_ref, mask_ref, bwd_ref, mid_ref, left_ref, right_ref, out_ref, du
+def _glue_kernel(g_ref, da_ref, db_ref, out_ref):
+    band = lax.axis_index("own")
+    even = lax.rem(band, 2) == 0
+    da = da_ref[...]
+    db = jnp.where((band == 1) | (band == 2), db_ref[...], 0.0)
+    above = jnp.where(even, db, da)
+    below = jnp.where(even, da, db)
+    out_ref[:FREQ] = g_ref[...]
+    out_ref[FREQ:] = pltpu.roll(jnp.where(_low_lanes((FREQ, 128)), below, above), 64, 1)
+
+
+def _stacked(val):
+    low = _low_lanes((FREQ, 128))
+    out = []
+    for r, (row, first) in enumerate(((32, True), (32, False), (0, True), (0, False))):
+        x = val[row : row + 32]
+        other = pltpu.roll(x, 64, 1)
+        dup = jnp.where(low, x, other) if first else jnp.where(low, other, x)
+        hi, lo = _split(dup)
+        out.append(jnp.where(low, hi.astype(F32), lo.astype(F32)).astype(BF))
+    return jnp.concatenate(out, 0)
+
+
+def _penalty(values):
+    values = values.astype(F32)
+    return GAMMA * 4.0 * values * (values * values - 1.0)
+
+
+def _store_du(du, part, lanes, m):
+    m = m.astype(BF)
+    du[part * 64 : part * 64 + 64, lanes] = m[:64]
+    du[128 + part * 64 : 128 + part * 64 + 64, lanes] = m[64:]
+
+
+def _middle_kernel(c_ref, mask_ref, bwd_ref, mid_ref, out_ref, du):
+    @pl.when(pl.program_id(0) == 0)
+    def _():
+        mid = _dot(_stacked(c_ref[...]), mid_ref[...])
+        for part in range(2):
+            _store_du(du, part, slice(0, 256), mid[:, part * 256 : part * 256 + 256])
+
+    out_ref[...] = _dot(bwd_ref[...], du[...]) + _penalty(mask_ref[...])
+
+
+def _sides_kernel(
+    done_ref, c_ref, a_ref, b_ref, mask_ref, bwd_ref, mid_ref, left_ref, right_ref, out_ref, du
 ):
-    @pl.when(pl.program_id(0) == 0)
+    @pl.when((pl.program_id(0) == 0) & (pl.program_id(1) == 0))
     def _():
         col = lax.axis_index("img")
         odd = lax.rem(col, 2) == 1
         a = a_ref[...]
         b = jnp.where((col > 0) & (col < 31), b_ref[...], 0.0)
-        left = jnp.where(odd, a, b)
-        right = jnp.where(odd, b, a)
-        low = _low_lanes((FREQ, 128))
-
-        def stacked(val):
-            out = []
-            for r, (row, first) in enumerate(((32, True), (32, False), (0, True), (0, False))):
-                x = val[row : row + 32]
-                other = pltpu.roll(x, 64, 1)
-                dup = jnp.where(low, x, other) if first else jnp.where(low, other, x)
-                hi, lo = _split(dup)
-                out.append(jnp.where(low, hi.astype(F32), lo.astype(F32)).astype(BF))
-            return jnp.concatenate(out, 0)
-
-        mid = _dot(stacked(c_ref[...]), mid_ref[...])
-        lo = _dot(stacked(left), left_ref[...])
-        hi = _dot(stacked(right), right_ref[...])
+        mid = _dot(_stacked(c_ref[...]), mid_ref[...])
+        left = _dot(_stacked(jnp.where(odd, a, b)), left_ref[...])
+        right = _dot(_stacked(jnp.where(odd, b, a)), right_ref[...])
         for part in range(2):
-            m = mid[:, part * 512 : part * 512 + 512]
-            m = jnp.concatenate(
-                [m[:, :128] + lo[:, part * 128 : part * 128 + 128], m[:, 128:384],
-                 m[:, 384:] + hi[:, part * 128 : part * 128 + 128]], 1
-            ).astype(BF)
-            du[part * 64 : part * 64 + 64, :] = m[:64]
-            du[128 + part * 64 : 128 + part * 64 + 64, :] = m[64:]
-
-    values = mask_ref[...].astype(F32)
-    penalty = GAMMA * 4.0 * values * (values * values - 1.0)
-    out_ref[...] = _dot(bwd_ref[...], du[...]) + penalty
+            at = part * 256
+            _store_du(du.at[0], part, slice(0, 128), mid[:, at : at + 128] + left[:, part * 128 : part * 128 + 128])
+            _store_du(du.at[1], part, slice(0, 128), mid[:, at + 128 : at + 256] + right[:, part * 128 : part * 128 + 128])
+
+    out_ref[...] = _dot(bwd_ref[...], du[pl.program_id(1)]) + _penalty(mask_ref[...])
 
 
 def _permute(value, target):
@@ -268,59 +300,54 @@
     return lax.ppermute(value, ("own", "img"), pairs)
 
 
-def _swap_even(i, n):
-    return i ^ 1
-
-
-def _swap_odd(i, n):
-    j = ((i + 1) ^ 1) - 1
-    return j if 0 <= j < n else i
-
-
 def _img_even(a, b):
-    return a, _swap_even(b, 32)
+    return a, b ^ 1
 
 
 def _img_odd(a, b):
-    return a, _swap_odd(b, 32)
+    c = ((b + 1) ^ 1) - 1
+    return (a, c) if 0 <= c < 32 else (a ^ 1, b)
 
 
 def _own_even(a, b):
-    return _swap_even(a, 4), b
+    return a ^ 1, b
 
 
 def _own_odd(a, b):
-    return _swap_odd(a, 4), b
+    c = ((a + 1) ^ 1) - 1
+    return (c, b) if 0 <= c < 4 else (a, b ^ 1)
 
 
 def on_device(mask_field, target_field, occupancy, kernels, weights):
     t = {name: jnp.asarray(value) for name, value in TABLES.items()}
-    band, col = lax.axis_index("own"), lax.axis_index("img")
     vmem = pl.BlockSpec(memory_space=pltpu.VMEM)
-    small = jax.ShapeDtypeStruct((64, 128), F32)
+    small = jax.ShapeDtypeStruct((FREQ, 128), F32)
+    limit = lambda mib: pltpu.CompilerParams(vmem_limit_bytes=mib << 20)
+
+    even = lax.rem(lax.axis_index("own"), 2) == 0
+    top, bottom = mask_field[:AMBIT], mask_field[2 * TILE - AMBIT :]
+    halo_a = _permute(jnp.where(even, bottom, top), _own_even)
+    halo_b = _permute(jnp.where(even, top, bottom), _own_odd)
 
     own, send_a, send_b = pl.pallas_call(
         _forward_kernel,
         out_shape=[small] * 3,
-        in_specs=[vmem] * 5,
+        in_specs=[vmem] * 8,
         out_specs=[vmem] * 3,
-        scratch_shapes=[pltpu.VMEM((256, 512), BF)],
+        scratch_shapes=[pltpu.VMEM((128, 512), BF)],
+        compiler_params=limit(8),
         name="forward",
-    )(mask_field, t["fwd"], t["f_mid"], t["f_left"], t["f_right"])
+    )(mask_field, halo_a, halo_b, t["fwd"], t["fwd_ambit"], t["f_mid"], t["f_left"], t["f_right"])
 
     wide = jnp.sqrt(weights)[:, None, None] * kernels
     kk = jnp.concatenate([wide[0], wide[0], wide[1], wide[1]], -1)
 
     got_a = _permute(send_a, _img_even)
     got_b = _permute(send_b, _img_odd)
-    x1 = own + got_a + jnp.where((col > 0) & (col < 31), got_b, 0.0)
-    even = lax.rem(band, 2) == 0
-    ua = _permute(jnp.where(even, x1[32:], x1[:32]), _own_even)
-    ub = _permute(jnp.where(even, x1[:32], x1[32:]), _own_odd)
 
     grads = pl.pallas_call(
         _image_kernel,
-        out_shape=jax.ShapeDtypeStruct((FREQ, 128), F32),
+        out_shape=small,
         in_specs=[vmem] * 5 + [pl.BlockSpec(memory_space=pltpu.SMEM)] + [vmem] * 8,
         out_specs=vmem,
         scratch_shapes=[
@@ -330,40 +357,69 @@
             pltpu.VMEM((2, KERNELS, FREQ, 256), BF),
             pltpu.VMEM((TILE, 128), BF),
         ],
+        compiler_params=limit(24),
         name="image",
     )(
-        x1, ua, ub, kk, target_field, occupancy,
+        own, got_a, got_b, kk, target_field, occupancy,
         t["tp"], t["te"], t["tx"], t["tv"], t["tz"], t["tw"], t["ty"], t["tg"],
     )
 
     da = _permute(grads, _own_even)
     db = _permute(grads, _own_odd)
-    inner = (band == 1) | (band == 2)
-    db = jnp.where(inner, db, 0.0)
-    above = jnp.where(even, db, da)
-    below = jnp.where(even, da, db)
-    center = jnp.concatenate([grads, jnp.concatenate([above[:, 64:], below[:, :64]], 1)], 0)
+    center = pl.pallas_call(
+        _glue_kernel,
+        out_shape=jax.ShapeDtypeStruct((2 * FREQ, 128), F32),
+        in_specs=[vmem] * 3,
+        out_specs=vmem,
+        compiler_params=limit(2),
+        name="glue",
+    )(grads, da, db)
     side_a = _permute(center, _img_even)
     side_b = _permute(center, _img_odd)
 
     rows = 256
-    whole = lambda shape: pl.BlockSpec(shape, lambda i: (0, 0))
+    result = jax.ShapeDtypeStruct((2 * TILE, TILE), F32)
+    whole = lambda *shape: pl.BlockSpec(shape, lambda *i: (0, 0))
+    b_mid = t["b_mid"]
+    cut = lambda lo, hi: [b_mid[:, lo:hi], b_mid[:, TILE + lo : TILE + hi]]
+    b_in = jnp.concatenate(cut(128, 384), 1)
+    b_out = jnp.concatenate([x for p in (0, TILE) for x in (b_mid[:, p : p + 128], b_mid[:, p + 384 : p + 512])], 1)
+    inside = pl.BlockSpec((pl.Element(rows), pl.Element(256)), lambda i: (i * rows, 128))
+    middle = pl.pallas_call(
+        _middle_kernel,
+        grid=(2 * TILE // rows,),
+        out_shape=result,
+        in_specs=[
+            whole(2 * FREQ, 128),
+            inside,
+            pl.BlockSpec((rows, 256), lambda i: (i, 0)),
+            whole(128, 512),
+        ],
+        out_specs=inside,
+        scratch_shapes=[pltpu.VMEM((256, 256), BF)],
+        compiler_params=limit(8),
+        name="middle",
+    )(center, mask_field, t["bwd"], b_in)
+    edge = pl.BlockSpec((rows, 128), lambda i, j: (i, 3 * j))
     return pl.pallas_call(
-        _backward_kernel,
-        grid=(2 * TILE // rows,),
-        out_shape=jax.ShapeDtypeStruct((2 * TILE, TILE), F32),
-        in_specs=[whole((64, 128))] * 3
+        _sides_kernel,
+        grid=(2 * TILE // rows, 2),
+        out_shape=result,
+        in_specs=[pl.BlockSpec(memory_space=pl.ANY)]
+        + [whole(2 * FREQ, 128)] * 3
         + [
-            pl.BlockSpec((rows, TILE), lambda i: (i, 0)),
-            pl.BlockSpec((rows, 256), lambda i: (i, 0)),
-            whole((128, 1024)),
-            whole((128, 256)),
-            whole((128, 256)),
+            edge,
+            pl.BlockSpec((rows, 256), lambda i, j: (i, 0)),
+            whole(128, 512),
+            whole(128, 256),
+            whole(128, 256),
         ],
-        out_specs=pl.BlockSpec((rows, TILE), lambda i: (i, 0)),
-        scratch_shapes=[pltpu.VMEM((256, TILE), BF)],
-        name="backward",
-    )(center, side_a, side_b, mask_field, t["bwd"], t["b_mid"], t["b_left"], t["b_right"])
+        out_specs=edge,
+        scratch_shapes=[pltpu.VMEM((2, 256, 128), BF)],
+        input_output_aliases={0: 0},
+        compiler_params=limit(8),
+        name="sides",
+    )(middle, center, side_a, side_b, mask_field, t["bwd"], b_out, t["b_left"], t["b_right"])
 
 
 def solution(mesh):

time: 45.8 us -> 31.5 us (0.69)
  starting transfers between devices: 14.1 us -> 7.23 us
  waiting for transfers between devices: 13 us -> 9.08 us
  Pallas kernels: 13.4 us -> 11.2 us
  local copies, waits for them, and re-layouts: 2.54 us -> 0.84 us
  other arithmetic: 2.13 us -> 2.63 us
    ppermute x8, starting transfers between devices: 14.1 us -> 7.23 us  [_permute(): return lax.ppermute(value, ('own', 'img'), pairs)]
    ppermute x8, waiting for transfers between devices: 13 us -> 9.08 us  [_permute(): return lax.ppermute(value, ('own', 'img'), pairs)]
    pallas_call x1, Pallas kernels: 2.76 us -> 0.52 us  [on_device(): pl.pallas_call(_forward_kernel, out_shape=[small] * 3, in_specs=[vmem] *...]
    unnamed x16 -> x42, local copies, waits for them, and re-layouts: 1.82 us -> 0.13 us
    mul x1, other arithmetic: 0.12 us -> 1.25 us  [on_device(): wide = jnp.sqrt(weights)[:, None, None] * kernels]
    select_n x3 -> x1, other arithmetic: 0.08 us -> 1.01 us  [on_device(): halo_b = _permute(jnp.where(even, top, bottom), _own_odd)]
    concatenate x1 -> x0, other arithmetic: 0.8 us -> none  [on_device(): jnp.concatenate([grads, jnp.concatenate([above[:, 64:], below[:, :64]], 1...]
    concatenate x1, other arithmetic: 1.12 us -> 0.37 us  [on_device(): kk = jnp.concatenate([wide[0], wide[0], wide[1], wide[1]], -1)]
  transfers between devices with their start and end apart: 8 -> 8, of which waited for: 6 -> 6; matrix products, arithmetic and copies ran while one was open for 4% -> 7% of each run, Pallas kernels for 0% -> 7%
where the time goes in v1:
time: 31.5 us; the launch traced here: 31.3 us
  Pallas kernels  11.2 us (36%)
  waiting for transfers between devices  9.08 us (29%)
  starting transfers between devices  7.23 us (23%)
  other arithmetic  2.63 us (8%)
  local copies, waits for them, and re-layouts  0.84 us (3%)
    ppermute x8, waiting for transfers between devices, _permute(): return lax.ppermute(value, ('own', 'img'), pairs)  9.08 us
    ppermute x8, starting transfers between devices, _permute(): return lax.ppermute(value, ('own', 'img'), pairs)  7.23 us
    pallas_call x1, Pallas kernels, on_device(): pl.pallas_call(_image_kernel, out_shape=small, in_specs=[vmem] * 5 + [pl....  4.32 us
    pallas_call x1, Pallas kernels, on_device(): pl.pallas_call(_sides_kernel, grid=(2 * TILE // rows, 2), out_shape=resul...  3.96 us
    pallas_call x1, Pallas kernels, on_device(): pl.pallas_call(_middle_kernel, grid=(2 * TILE // rows,), out_shape=result...  2.31 us
    mul x1, other arithmetic, on_device(): wide = jnp.sqrt(weights)[:, None, None] * kernels  1.25 us
    select_n x1, other arithmetic, on_device(): halo_b = _permute(jnp.where(even, top, bottom), _own_odd)  1.01 us
    sqrt x1, local copies, waits for them, and re-layouts, on_device(): wide = jnp.sqrt(weights)[:, None, None] * kernels  0.66 us
  transfers between devices with their start and end apart: 8, of which 6 were waited for; matrix products, arithmetic and copies ran while one was open for 7% of the time, Pallas kernels for 7%

profile of v1, /device:TPU:36, one launch (start us, length us, event | category | flops | bytes accessed | tf_op | source)
XLA Modules:
  0.0 31.3 jit_solution(561637878577805779)
XLA Ops:
  0.0 0.0 copy-start.18
  0.0 0.0 copy-start.5
  0.1 1.0 %broadcast_select_fusion = (bf16[64,512]{1,0:T(8,128)(2,1)S(1)}, bf16[64,512]{1,0:T(8,128)(2,1)S(1)}) fusion(pred[]{:T(512)S(6)} %eq.3, bf16[1024,512]{1,0:T(8,128)(2,1)} %mask_ref.5), kind=kLoop, calls=%fused_computation.4 | loop fusion | flops 65536 | bytes 262145 | tf_op jit(solution)/shard_map/jit(_where)/select_n | solution.py:330
  1.1 2.0 %collective-permute-start.1 = (bf16[64,512]{1,0:T(8,128)(2,1)S(1)}, bf16[64,512]{1,0:T(8,128)(2,1)S(1)}, u32[]{:S(2)}, u32[]{:S(2)}) collective-permute-start(bf16[64,512]{1,0:T(8,128)(2,1)S(1)} %get-tuple-element.11), channel_id=1, source_target_pairs={{0,1},{1,0},{2,3},{3,2},{4,5},{5,4},{6,7},{7,6},{8,9},{9,8},{10,11... | collective-permute-start | bytes 196616 | tf_op jit(solution)/shard_map/ppermute | solution.py:300
  3.1 0.7 %sqrt.3 = f32[24]{0:T(128)S(1)} sqrt(f32[24]{0:T(128)} %param.26) | non-fusion elementwise | bytes 192 | tf_op jit(solution)/shard_map/sqrt | solution.py:342
  3.7 1.3 %broadcast_multiply_fusion = f32[2,24,32,32]{3,2,1,0:T(8,128)S(1)} fusion(f32[2,24,32,32]{3,2,1,0:T(8,128)} %param.25, f32[24]{0:T(128)S(1)} %sqrt.3), kind=kLoop, calls=%fused_computation.3 | loop fusion | flops 49152 | bytes 393312 | tf_op jit(solution)/shard_map/mul | solution.py:342
  5.0 0.0 copy-start.3
  5.1 0.1 slice_bitcast_fusion.1
  5.2 0.2 collective-permute-done.1.hb_ref
  5.4 1.9 %collective-permute-done.ha_ref = bf16[64,512]{1,0:T(8,128)(2,1)S(1)} collective-permute-done((bf16[64,512]{1,0:T(8,128)(2,1)S(1)}, bf16[64,512]{1,0:T(8,128)(2,1)S(1)}, u32[]{:S(2)}, u32[]{:S(2)}) %collective-permute-start) | collective-permute-done | bytes 65568 | tf_op jit(solution)/shard_map/ppermute | solution.py:300
  7.4 0.5 %forward.1 = (f32[32,128]{1,0:T(8,128)S(1)}, f32[32,128]{1,0:T(8,128)S(1)}, f32[32,128]{1,0:T(8,128)S(1)}) custom-call(bf16[1024,512]{1,0:T(8,128)(2,1)S(1)} %copy-done, bf16[64,512]{1,0:T(8,128)(2,1)S(1)} %collective-permute-done.ha_ref, bf16[64,512]{1,0:T(8,128)(2,1)S(1)} %collective-permute-done.1.hb_ref, bf16[128,1024]{1,0:T(8,128)(2,1)S(1)} %copy-done.5, ...), custom_call_target="tpu_custom_call" | custom-call | tf_op jit(solution)/shard_map/forward/pallas_call | solution.py:332
  7.9 0.1 collective-permute-start.2
  8.0 3.1 %collective-permute-start.3 = (f32[32,128]{1,0:T(8,128)S(1)}, f32[32,128]{1,0:T(8,128)S(1)}, u32[]{:S(2)}, u32[]{:S(2)}) collective-permute-start(f32[32,128]{1,0:T(8,128)S(1)} %get-tuple-element.10), channel_id=1, source_target_pairs={{0,32},{1,2},{2,1},{3,4},{4,3},{5,6},{6,5},{7,8},{8,7},{9,10},{10,... | collective-permute-start | bytes 49160 | tf_op jit(solution)/shard_map/ppermute | solution.py:300
  11.1 0.4 %pad_maximum_fusion.kk_ref = f32[24,32,128]{2,1,0:T(8,128)S(1)} fusion(f32[24,32,32]{2,1,0:T(8,128)S(1)} %get-tuple-element.14, f32[24,32,32]{2,1,0:T(8,128)S(1)} %get-tuple-element.13), kind=kLoop, calls=%fused_computation.2 | loop fusion | flops 294912 | bytes 589824 | tf_op jit(solution)/shard_map/concatenate | solution.py:343
  11.5 1.9 %collective-permute-done.3.xb_ref = f32[32,128]{1,0:T(8,128)S(1)} collective-permute-done((f32[32,128]{1,0:T(8,128)S(1)}, f32[32,128]{1,0:T(8,128)S(1)}, u32[]{:S(2)}, u32[]{:S(2)}) %collective-permute-start.3) | collective-permute-done | bytes 16416 | tf_op jit(solution)/shard_map/ppermute | solution.py:300
  13.4 4.3 %image.1.g_ref = f32[32,128]{1,0:T(8,128)S(1)} custom-call(f32[32,128]{1,0:T(8,128)S(1)} %get-tuple-element.8.x_ref, f32[32,128]{1,0:T(8,128)S(1)} %collective-permute-done.2.xa_ref, f32[32,128]{1,0:T(8,128)S(1)} %collective-permute-done.3.xb_ref, f32[24,32,128]{2,1,0:T(8,128)S(1)} %pad_maximum_fusion.kk_ref, bf16[1024,512]{1,0:T(8,128)(2,1)S(1)} %copy-done.2, ...), custom_call_target="tpu_custom_call" | custom-call | tf_op jit(solution)/shard_map/image/pallas_call | solution.py:348
  17.8 0.2 collective-permute-start.5
  18.0 3.6 %collective-permute-done.5.db_ref = f32[32,128]{1,0:T(8,128)S(1)} collective-permute-done((f32[32,128]{1,0:T(8,128)S(1)}, f32[32,128]{1,0:T(8,128)S(1)}, u32[]{:S(2)}, u32[]{:S(2)}) %collective-permute-start.5) | collective-permute-done | bytes 16416 | tf_op jit(solution)/shard_map/ppermute | solution.py:300
  21.6 0.1 collective-permute-done.4.da_ref
  21.8 0.1 glue.1.c_ref
  21.8 1.8 %collective-permute-start.7 = (f32[64,128]{1,0:T(8,128)S(1)}, f32[64,128]{1,0:T(8,128)S(1)}, u32[]{:S(2)}, u32[]{:S(2)}) collective-permute-start(f32[64,128]{1,0:T(8,128)S(1)} %glue.1.c_ref), channel_id=1, source_target_pairs={{0,32},{1,2},{2,1},{3,4},{4,3},{5,6},{6,5},{7,8},{8,7},{9,10},{10,... | collective-permute-start | bytes 98312 | tf_op jit(solution)/shard_map/ppermute | solution.py:300
  23.7 2.3 %middle.1.done_ref = f32[1024,512]{1,0:T(8,128)} custom-call(f32[64,128]{1,0:T(8,128)S(1)} %glue.1.c_ref, bf16[1024,512]{1,0:T(8,128)(2,1)S(1)} %copy-done, bf16[1024,256]{1,0:T(8,128)(2,1)S(1)} %copy-done.1, bf16[128,512]{1,0:T(8,128)(2,1)S(1)} %copy-done.11), custom_call_target="tpu_custom_call" | custom-call | tf_op jit(solution)/shard_map/middle/pallas_call | solution.py:388
  26.0 1.3 %collective-permute-done.7.b_ref = f32[64,128]{1,0:T(8,128)S(1)} collective-permute-done((f32[64,128]{1,0:T(8,128)S(1)}, f32[64,128]{1,0:T(8,128)S(1)}, u32[]{:S(2)}, u32[]{:S(2)}) %collective-permute-start.7) | collective-permute-done | bytes 32800 | tf_op jit(solution)/shard_map/ppermute | solution.py:300
  27.3 4.0 %sides.1 = f32[1024,512]{1,0:T(8,128)} custom-call(f32[1024,512]{1,0:T(8,128)} %middle.1.done_ref, f32[64,128]{1,0:T(8,128)S(1)} %glue.1.c_ref, f32[64,128]{1,0:T(8,128)S(1)} %collective-permute-done.6.a_ref, f32[64,128]{1,0:T(8,128)S(1)} %collective-permute-done.7.b_ref, bf16[1024,512]{1,0:T(8,128)(2,1)S(1)} %copy-done, ...), custom_call_target="tpu_custom_call", output_to_operand_aliasing={{}: (0, {})} | custom-call | tf_op jit(solution)/shard_map/sides/pallas_call | solution.py:404
  (44 shorter events, 0.1 us)
Async XLA Ops:
  0.0 7.3 %copy-start.18 = (bf16[128,128]{1,0:T(8,128)(2,1)S(1)}, bf16[128,128]{1,0:T(8,128)(2,1)}, u32[]{:S(2)}) copy-start(bf16[128,128]{1,0:T(8,128)(2,1)} %constant.47.clone.ambit_ref) | copy-start | bytes 98308
  1.1 4.3 %collective-permute-start.1 = (bf16[64,512]{1,0:T(8,128)(2,1)S(1)}, bf16[64,512]{1,0:T(8,128)(2,1)S(1)}, u32[]{:S(2)}, u32[]{:S(2)}) collective-permute-start(bf16[64,512]{1,0:T(8,128)(2,1)S(1)} %get-tuple-element.11), channel_id=1, source_target_pairs={{0,1},{1,0},{2,3},{3,2},{4,5},{5,4},{6,7},{7,6},{8,9},{9,8},{10,11... | collective-permute-start | bytes 196616 | tf_op jit(solution)/shard_map/ppermute | solution.py:300
  3.1 4.3 %collective-permute-start = (bf16[64,512]{1,0:T(8,128)(2,1)S(1)}, bf16[64,512]{1,0:T(8,128)(2,1)S(1)}, u32[]{:S(2)}, u32[]{:S(2)}) collective-permute-start(bf16[64,512]{1,0:T(8,128)(2,1)S(1)} %get-tuple-element.12), channel_id=1, source_target_pairs={{0,32},{1,33},{2,34},{3,35},{4,36},{5,37},{6,38},{7,39},{8,40},{9,... | collective-permute-start | bytes 196616 | tf_op jit(solution)/shard_map/ppermute | solution.py:300
  5.0 8.4 %copy-start.2 = (bf16[1024,512]{1,0:T(8,128)(2,1)S(1)}, bf16[1024,512]{1,0:T(8,128)(2,1)}, u32[]{:S(2)}) copy-start(bf16[1024,512]{1,0:T(8,128)(2,1)} %target_ref.1) | copy-start | bytes 3145732
  5.0 8.4 %copy-start.3 = (bf16[384,512]{1,0:T(8,128)(2,1)S(1)}, bf16[384,512]{1,0:T(8,128)(2,1)}, u32[]{:S(2)}) copy-start(bf16[384,512]{1,0:T(8,128)(2,1)} %constant.59.clone.tz_ref) | copy-start | bytes 1179652
  5.0 8.4 %copy-start.6 = (bf16[512,256]{1,0:T(8,128)(2,1)S(1)}, bf16[512,256]{1,0:T(8,128)(2,1)}, u32[]{:S(2)}) copy-start(bf16[512,256]{1,0:T(8,128)(2,1)} %constant.61.clone.ty_ref) | copy-start | bytes 786436
  5.0 8.4 %copy-start.7 = (bf16[512,192]{1,0:T(8,128)(2,1)S(1)}, bf16[512,192]{1,0:T(8,128)(2,1)}, u32[]{:S(2)}) copy-start(bf16[512,192]{1,0:T(8,128)(2,1)} %constant.60.clone.tw_ref) | copy-start | bytes 589828
  5.0 8.4 %copy-start.8 = (bf16[384,256]{1,0:T(8,128)(2,1)S(1)}, bf16[384,256]{1,0:T(8,128)(2,1)}, u32[]{:S(2)}) copy-start(bf16[384,256]{1,0:T(8,128)(2,1)} %constant.55.clone.tp_ref) | copy-start | bytes 589828
  5.0 8.4 %copy-start.10 = (bf16[128,512]{1,0:T(8,128)(2,1)S(1)}, bf16[128,512]{1,0:T(8,128)(2,1)}, u32[]{:S(2)}) copy-start(bf16[128,512]{1,0:T(8,128)(2,1)} %constant.62.clone.tg_ref) | copy-start | bytes 393220
  5.1 8.3 %copy-start.14 = (bf16[256,128]{1,0:T(8,128)(2,1)S(1)}, bf16[256,128]{1,0:T(8,128)(2,1)}, u32[]{:S(2)}) copy-start(bf16[256,128]{1,0:T(8,128)(2,1)} %constant.58.clone.tv_ref) | copy-start | bytes 196612
  5.1 8.3 %copy-start.17 = (bf16[64,192]{1,0:T(8,128)(2,1)S(1)}, bf16[64,192]{1,0:T(8,128)(2,1)}, u32[]{:S(2)}) copy-start(bf16[64,192]{1,0:T(8,128)(2,1)} %constant.56.clone.te_ref) | copy-start | bytes 73732
  5.1 8.3 %copy-start.19 = (bf16[64,64]{1,0:T(8,128)(2,1)S(1)}, bf16[64,64]{1,0:T(8,128)(2,1)}, u32[]{:S(2)}) copy-start(bf16[64,64]{1,0:T(8,128)(2,1)} %constant.57.clone.tx_ref) | copy-start | bytes 24580
  5.1 8.3 %copy-start.20 = (s32[8,32]{1,0:T(8,128)S(1)}, s32[8,32]{1,0:T(8,128)}, u32[]{:S(2)}) copy-start(s32[8,32]{1,0:T(8,128)} %occ_ref.1) | copy-start | bytes 3076
  7.9 15.8 %copy-start.1 = (bf16[1024,256]{1,0:T(8,128)(2,1)S(1)}, bf16[1024,256]{1,0:T(8,128)(2,1)}, u32[]{:S(2)}) copy-start(bf16[1024,256]{1,0:T(8,128)(2,1)} %constant.48.clone.bwd_ref) | copy-start | bytes 1572868
  7.9 15.8 %copy-start.11 = (bf16[128,512]{1,0:T(8,128)(2,1)S(1)}, bf16[128,512]{1,0:T(8,128)(2,1)}, u32[]{:S(2)}) copy-start(bf16[128,512]{1,0:T(8,128)(2,1)} %constant.65.mid_ref) | copy-start | bytes 393220
  7.9 3.6 %collective-permute-start.2 = (f32[32,128]{1,0:T(8,128)S(1)}, f32[32,128]{1,0:T(8,128)S(1)}, u32[]{:S(2)}, u32[]{:S(2)}) collective-permute-start(f32[32,128]{1,0:T(8,128)S(1)} %get-tuple-element.9), channel_id=1, source_target_pairs={{0,1},{1,0},{2,3},{3,2},{4,5},{5,4},{6,7},{7,6},{8,9},{9,8},{10,11... | collective-permute-start | bytes 49160 | tf_op jit(solution)/shard_map/ppermute | solution.py:300
  8.0 5.4 %collective-permute-start.3 = (f32[32,128]{1,0:T(8,128)S(1)}, f32[32,128]{1,0:T(8,128)S(1)}, u32[]{:S(2)}, u32[]{:S(2)}) collective-permute-start(f32[32,128]{1,0:T(8,128)S(1)} %get-tuple-element.10), channel_id=1, source_target_pairs={{0,32},{1,2},{2,1},{3,4},{4,3},{5,6},{6,5},{7,8},{8,7},{9,10},{10,... | collective-permute-start | bytes 49160 | tf_op jit(solution)/shard_map/ppermute | solution.py:300
  17.8 9.5 %copy-start.9 = (bf16[128,512]{1,0:T(8,128)(2,1)S(1)}, bf16[128,512]{1,0:T(8,128)(2,1)}, u32[]{:S(2)}) copy-start(bf16[128,512]{1,0:T(8,128)(2,1)} %constant.69.mid_ref) | copy-start | bytes 393220
  17.8 9.5 %copy-start.12 = (bf16[128,256]{1,0:T(8,128)(2,1)S(1)}, bf16[128,256]{1,0:T(8,128)(2,1)}, u32[]{:S(2)}) copy-start(bf16[128,256]{1,0:T(8,128)(2,1)} %constant.54.clone.right_ref) | copy-start | bytes 196612
  17.8 9.5 %copy-start.13 = (bf16[128,256]{1,0:T(8,128)(2,1)S(1)}, bf16[128,256]{1,0:T(8,128)(2,1)}, u32[]{:S(2)}) copy-start(bf16[128,256]{1,0:T(8,128)(2,1)} %constant.52.clone.left_ref) | copy-start | bytes 196612
  17.8 3.8 %collective-permute-start.5 = (f32[32,128]{1,0:T(8,128)S(1)}, f32[32,128]{1,0:T(8,128)S(1)}, u32[]{:S(2)}, u32[]{:S(2)}) collective-permute-start(f32[32,128]{1,0:T(8,128)S(1)} %image.1.g_ref), channel_id=1, source_target_pairs={{0,1},{1,0},{2,3},{3,2},{4,5},{5,4},{6,7},{7,6},{8,9},{9,8},{10,11... | collective-permute-start | bytes 49160 | tf_op jit(solution)/shard_map/ppermute | solution.py:300
  18.0 3.7 %collective-permute-start.4 = (f32[32,128]{1,0:T(8,128)S(1)}, f32[32,128]{1,0:T(8,128)S(1)}, u32[]{:S(2)}, u32[]{:S(2)}) collective-permute-start(f32[32,128]{1,0:T(8,128)S(1)} %image.1.g_ref), channel_id=1, source_target_pairs={{0,32},{1,33},{2,34},{3,35},{4,36},{5,37},{6,38},{7,39},{8,40},{9,... | collective-permute-start | bytes 49160 | tf_op jit(solution)/shard_map/ppermute | solution.py:300
  21.8 5.5 %collective-permute-start.7 = (f32[64,128]{1,0:T(8,128)S(1)}, f32[64,128]{1,0:T(8,128)S(1)}, u32[]{:S(2)}, u32[]{:S(2)}) collective-permute-start(f32[64,128]{1,0:T(8,128)S(1)} %glue.1.c_ref), channel_id=1, source_target_pairs={{0,32},{1,2},{2,1},{3,4},{4,3},{5,6},{6,5},{7,8},{8,7},{9,10},{10,... | collective-permute-start | bytes 98312 | tf_op jit(solution)/shard_map/ppermute | solution.py:300
  23.7 3.6 %collective-permute-start.6 = (f32[64,128]{1,0:T(8,128)S(1)}, f32[64,128]{1,0:T(8,128)S(1)}, u32[]{:S(2)}, u32[]{:S(2)}) collective-permute-start(f32[64,128]{1,0:T(8,128)S(1)} %glue.1.c_ref), channel_id=1, source_target_pairs={{0,1},{1,0},{2,3},{3,2},{4,5},{5,4},{6,7},{7,6},{8,9},{9,8},{10,11... | collective-permute-start | bytes 98312 | tf_op jit(solution)/shard_map/ppermute | solution.py:300
  (5 other events, 36.6 us)

commit v2 on v1

v2 whole, which is shorter than its diff:
```python
import jax
import jax.numpy as jnp
import numpy as np
from jax import lax
from jax.experimental import pallas as pl
from jax.experimental.pallas import tpu as pltpu
from jax.sharding import PartitionSpec as P

TILE = 512
AMBIT = 64
FREQ = 32
KERNELS = 24
PAD = 640
GRID = 64

STEEP = 2.0
THRESHOLD = 1.5
GAMMA = 0.25

BF = jnp.bfloat16
F32 = jnp.float32


def _bf(x):
    return np.asarray(x, np.float32).astype(BF)


def _hi_lo(x):
    hi = _bf(x)
    return hi, _bf(np.asarray(x, np.float64) - hi.astype(np.float64))


def _build_tables():
    f = np.arange(FREQ) - FREQ // 2
    ang = 2 * np.pi * ((f[:, None] * np.arange(PAD)[None]) % PAD) / PAD
    c = _bf(np.cos(ang) / np.sqrt(PAD)).astype(np.float64)
    s = _bf(-np.sin(ang) / np.sqrt(PAD)).astype(np.float64)

    height, width = 2 * TILE, TILE

    def rows_of(table, first, lo, hi):
        out = np.zeros((FREQ, hi - lo))
        y = np.arange(lo, hi) + first
        ok = (y >= 0) & (y < PAD)
        out[:, ok] = table[:, y[ok]]
        return out

    own_rows = [
        np.concatenate([rows_of(tb, first, 0, height), rows_of(tb, first, -AMBIT, 0), rows_of(tb, first, height, height + AMBIT)], 1)
        for first in (AMBIT, AMBIT - TILE)
        for tb in (c, s)
    ]
    fwd = np.concatenate(own_rows, 0)
    first = {0: AMBIT + TILE, 1: AMBIT, 2: AMBIT - TILE, 3: AMBIT - 2 * TILE}
    bwd = np.concatenate([rows_of(tb, first[r], 0, height) for tb in (c, s) for r in (1, 2)], 0)
    far = np.concatenate(
        [
            np.concatenate([rows_of(tb, first[0], 0, AMBIT).T for tb in (c, s)], 1),
            np.concatenate([rows_of(tb, first[3], height - AMBIT, height).T for tb in (c, s)], 1),
        ],
        0,
    )

    def cols_of(table, shift, lo, hi):
        out = np.zeros((FREQ, hi - lo))
        x = np.arange(lo, hi) + shift
        ok = (x >= 0) & (x < PAD)
        out[:, ok] = table[:, x[ok]]
        return out

    t = {"fwd": _bf(fwd[:, :height]), "fwd_ambit": _bf(fwd[:, height:]), "bwd": _bf(bwd.T), "far": _bf(far)}
    ranges = {"mid": (AMBIT, 0, width), "left": (AMBIT + TILE, 0, 128), "right": (AMBIT - TILE, width - 128, width)}
    for name, (shift, lo, hi) in ranges.items():
        cc, ss = cols_of(c, shift, lo, hi), cols_of(s, shift, lo, hi)
        re = np.concatenate([cc.T, ss.T], 1)
        im = np.concatenate([-ss.T, cc.T], 1)
        both = np.concatenate([re, im], 0)
        t["f_" + name] = _bf(np.concatenate([both, both], 1))
        dre, dim = np.concatenate([cc, ss], 0), np.concatenate([-ss, cc], 0)
        t["b_" + name] = _bf(np.concatenate([np.concatenate([dre, dre], 0), np.concatenate([dim, dim], 0)], 1))

    side = np.concatenate([t.pop("b_left"), t.pop("b_right")], 0)
    t["b_side"] = side

    grid = np.arange(GRID) * (PAD // GRID)
    hang = 2 * np.pi * ((grid[:, None] * f[None]) % PAD) / PAD
    hc, hs = np.cos(hang) / np.sqrt(FREQ), np.sin(hang) / np.sqrt(FREQ)
    tp = np.concatenate(
        [
            np.concatenate([hc.T, hs.T, -hs.T, hc.T], 1),
            np.concatenate([-hs.T, hc.T, -hc.T, -hs.T], 1),
        ],
        0,
    )
    hi, lo = _hi_lo(tp)
    t["tp"] = np.concatenate([hi, hi, lo, lo], 0)
    hi, lo = _hi_lo(np.concatenate([hc, hs], 1))
    t["te"] = np.concatenate([hi, lo], 1)
    t["tx"] = hi.T.copy()
    v1 = np.block([[hc, -hs], [hs, hc]])
    v2 = np.block([[-hs, -hc], [hc, -hs]])
    v = np.concatenate([v1, v2], 0)
    t["tv"] = _bf(np.concatenate([v, v[:, FREQ:], -v[:, :FREQ]], 1))

    n = np.arange(1 - FREQ, FREQ)
    y = np.arange(TILE) + AMBIT
    w = np.cos(2 * np.pi * ((y[:, None, None] - grid[None, :, None]) * n[None, None, :] % PAD) / PAD).sum(-1) / GRID
    hi, lo = _hi_lo(w)
    t["tz"] = np.concatenate([hi.T, hi.T, hi.T, hi.T, lo.T, lo.T], 0)
    t["tw"] = np.concatenate([hi, hi, lo, np.ones((TILE, 1), BF), np.zeros((TILE, 15), BF)], 1)
    t["ty"] = np.concatenate([hi, hi, lo, lo], 1)
    t["tg"] = np.concatenate([hi.T, lo.T], 0)
    return t


TABLES = _build_tables()


def _dot(a, b):
    return jnp.dot(a, b, preferred_element_type=F32)


def _split(x):
    hi = x.astype(BF)
    return hi, (x - hi.astype(F32)).astype(BF)


def _low_lanes(shape):
    return lax.broadcasted_iota(jnp.int32, shape, len(shape) - 1) < 64


def _forward_kernel(
    mask_ref, ha_ref, hb_ref, fwd_ref, ambit_ref, mid_ref, left_ref, right_ref, own_ref, a_ref, b_ref, acc
):
    band = lax.axis_index("own")
    even = lax.rem(band, 2) == 0
    inner = (band == 1) | (band == 2)
    odd = lax.rem(lax.axis_index("img"), 2) == 1
    ha = ha_ref[...].astype(F32)
    hb = jnp.where(inner, hb_ref[...].astype(F32), 0.0)
    ambit = jnp.concatenate([jnp.where(even, hb, ha), jnp.where(even, ha, hb)], 0).astype(BF)
    acc[...] = (_dot(fwd_ref[...], mask_ref[...]) + _dot(ambit_ref[...], ambit)).astype(BF)

    def project(lo, hi, table):
        lhs = jnp.concatenate(
            [
                jnp.concatenate([acc[0:32, lo:hi], acc[32:64, lo:hi]], 1),
                jnp.concatenate([acc[64:96, lo:hi], acc[96:128, lo:hi]], 1),
            ],
            0,
        )
        out = _dot(lhs, table[...])
        return jnp.where(_low_lanes((FREQ, 128)), out[:FREQ], out[FREQ:])

    own_ref[...] = project(0, 512, mid_ref)
    left = project(0, 128, left_ref)
    right = project(384, 512, right_ref)
    a_ref[...] = jnp.where(odd, left, right)
    b_ref[...] = jnp.where(odd, right, left)


def _image_kernel(
    x_ref, xa_ref, xb_ref, kk_ref, target_ref, occ_ref,
    tp_ref, te_ref, tx_ref, tv_ref, tz_ref, tw_ref, ty_ref, tg_ref,
    out_ref, p_hi, fields, xs, yb,
):
    band, col = lax.axis_index("own"), lax.axis_index("img")
    m = x_ref[...] + xa_ref[...] + jnp.where((col > 0) & (col < 31), xb_ref[...], 0.0)
    turned = pltpu.roll(m, 64, 1)
    low = _low_lanes((FREQ, 128))
    lane = lax.broadcasted_iota(jnp.int32, (FREQ, 128), 1)

    kk = kk_ref[...]
    for t in range(2):
        dup = jnp.where(low, m, turned) if t == 0 else jnp.where(low, turned, m)
        swapped = pltpu.roll(dup, 32, 1)
        swapped = jnp.where(lane < 96, -swapped, swapped)
        m4 = jnp.where(low, dup, swapped)
        prod = kk * m4[None]
        prod = prod.reshape(KERNELS * FREQ, 128).astype(BF)
        half = _dot(jnp.concatenate([prod, prod], 1), tp_ref[...])
        p_hi[t] = half.astype(BF).reshape(KERNELS, FREQ, 256)

    total = jnp.zeros((GRID, 256), F32)
    for k in range(KERNELS):
        def halves(ref):
            return jnp.concatenate(
                [
                    jnp.concatenate([ref[0, k, :, :128], ref[1, k, :, :128]], 1),
                    jnp.concatenate([ref[0, k, :, 128:], ref[1, k, :, 128:]], 1),
                ],
                0,
            )
        hi = halves(p_hi)
        e = _dot(te_ref[...], jnp.concatenate([hi, hi], 0))
        fields[k] = e
        total = total + e * e

    hi, lo = _split(jnp.concatenate([total[:, :128], total[:, 128:]], 0))
    z = _dot(jnp.concatenate([hi, lo, hi], 1), tz_ref[...])
    pulls = []
    rows = 128
    for t in range(2):
        hi, lo = _split(z[t * GRID : (t + 1) * GRID])
        stack = jnp.concatenate([hi, lo, hi, jnp.full((16, TILE), -THRESHOLD, BF)], 0)
        for c in range(TILE // rows):
            at = c * rows
            over = _dot(tw_ref[at : at + rows], stack)
            th = jnp.tanh((0.5 * STEEP) * over)
            sens = ((th + 1.0) - 2.0 * target_ref[t * TILE + at : t * TILE + at + rows, :].astype(F32)) * (1.0 - th * th)
            y = _dot(sens.astype(BF), ty_ref[...])
            yb[at : at + rows, :] = (y[:, :128] + y[:, 128:]).astype(BF)
        g = _dot(tg_ref[...], yb[...])
        pulls.append((0.5 * STEEP) * (g[:GRID] + g[GRID:]))
    pull = jnp.concatenate(pulls, 1)

    for k in range(KERNELS):
        q = (pull * fields[k]).astype(BF)
        x = _dot(tx_ref[...], q).astype(BF)
        for t in range(2):
            at = t * 128
            xs[t, k] = jnp.concatenate([x[:32, at : at + 128], x[32:, at : at + 128]], 1)

    d = _dot(xs[...].reshape(2 * KERNELS * FREQ, 256), tv_ref[...])
    d = d.reshape(2, KERNELS, FREQ, 128)
    parts = []
    for t in range(2):
        s = jnp.sum(kk * d[t], 0)
        s = s + pltpu.roll(s, 64, 1)
        parts.append(jnp.where(occ_ref[2 * band + t, col] > 0, s, 0.0))
    out_ref[...] = jnp.where(low, parts[0], parts[1])


def _glue_kernel(done_ref, g_ref, sa_ref, sb_ref, ta_ref, tb_ref):
    even = lax.rem(lax.axis_index("own"), 2) == 0
    low = _low_lanes((FREQ, 128))
    own = g_ref[...]
    left, right = _by_side(sa_ref, sb_ref)
    turn = lambda x: pltpu.roll(x, 64, 1)
    first = jnp.concatenate([jnp.where(low, own, turn(left)), jnp.where(low, right, 0.0)], 0)
    second = jnp.concatenate([jnp.where(low, turn(own), left), jnp.where(low, turn(right), 0.0)], 0)
    ta_ref[...] = jnp.where(even, second, first)
    tb_ref[...] = jnp.where(even, first, second)


def _by_side(sa_ref, sb_ref):
    col = lax.axis_index("img")
    odd = lax.rem(col, 2) == 1
    a = sa_ref[...]
    b = jnp.where((col > 0) & (col < 31), sb_ref[...], 0.0)
    return jnp.where(odd, a, b), jnp.where(odd, b, a)


def _spread(val, which):
    low = _low_lanes((FREQ, 128))
    other = pltpu.roll(val, 64, 1)
    dup = jnp.where(low, val, other) if which == 0 else jnp.where(low, other, val)
    hi, lo = _split(dup)
    return jnp.where(low, hi.astype(F32), lo.astype(F32)).astype(BF)


def _stacked(val):
    return jnp.concatenate([_spread(val, 0), _spread(val, 1)], 0)


def _penalty(values):
    values = values.astype(F32)
    return GAMMA * 4.0 * values * (values * values - 1.0)


ROWS = 256
CHUNKS = tuple((i * ROWS + (AMBIT if i == 0 else 0), (i + 1) * ROWS - (AMBIT if i == 3 else 0)) for i in range(4))


def _inner_kernel(g_ref, mask_ref, bwd_ref, mid_ref, out_ref, edge_ref, rim_ref, du, staged, sem):
    mid = _dot(_stacked(g_ref[...]), mid_ref[...]).astype(BF)
    du[:64] = mid[:, :TILE]
    du[64:] = mid[:, TILE:]
    copies = []
    for i, (lo, hi) in enumerate(CHUNKS):
        rows = pl.ds(i * ROWS, ROWS)
        g = _dot(bwd_ref[rows, :], du[...]) + _penalty(mask_ref[rows, :])
        staged[rows, :] = g[:, 128:384]
        copy = pltpu.make_async_copy(
            staged.at[pl.ds(lo, hi - lo)], out_ref.at[pl.ds(lo, hi - lo), pl.ds(128, 256)], sem.at[i]
        )
        copy.start()
        copies.append(copy)
        edge_ref[rows, :128] = g[:, :128]
        edge_ref[rows, 128:] = g[:, 384:]
        if i == 0:
            rim_ref[:AMBIT] = g[:AMBIT, 128:384]
        if i == 3:
            rim_ref[AMBIT:] = g[ROWS - AMBIT :, 128:384]
    for copy in copies:
        copy.wait()


def _sides_kernel(done_ref, edge_ref, rim_ref, sa_ref, sb_ref, bwd_ref, side_ref, out_ref, part_ref, du, staged, sem):
    left, right = _by_side(sa_ref, sb_ref)
    lhs = jnp.concatenate([_stacked(left), _stacked(right)], 1)
    both = _dot(lhs, side_ref[...]).astype(BF)
    du[:64] = both[:, :128]
    du[64:] = both[:, 128:]
    low = _low_lanes((ROWS, 128))
    part_ref[:, 128:384] = rim_ref[...]
    copies = []
    for i, (lo, hi) in enumerate(CHUNKS):
        rows = pl.ds(i * ROWS, ROWS)
        g = _dot(bwd_ref[rows, :], du[...])
        for side in range(2):
            lanes = pl.ds(side * 128, 128)
            whole = edge_ref[rows, lanes] + (jnp.where(low, g, 0.0) if side == 0 else jnp.where(low, 0.0, g))
            staged[rows, lanes] = whole
            copy = pltpu.make_async_copy(
                staged.at[pl.ds(lo, hi - lo), lanes],
                out_ref.at[pl.ds(lo, hi - lo), pl.ds(side * 384, 128)],
                sem.at[2 * i + side],
            )
            copy.start()
            copies.append(copy)
            if i == 0:
                part_ref[:AMBIT, side * 384 : side * 384 + 128] = whole[:AMBIT]
            if i == 3:
                part_ref[AMBIT:, side * 384 : side * 384 + 128] = whole[ROWS - AMBIT :]
    for copy in copies:
        copy.wait()


def _rims_kernel(done_ref, part_ref, ta_ref, tb_ref, far_ref, mid_ref, side_ref, out_ref, staged, sem):
    band = lax.axis_index("own")
    even = lax.rem(band, 2) == 0
    ta = ta_ref[...]
    tb = jnp.where((band == 1) | (band == 2), tb_ref[...], 0.0)
    own, near = [], []
    for got in (jnp.where(even, tb, ta), jnp.where(even, ta, tb)):
        own.append(_spread(got[:FREQ], 0))
        near.append(jnp.concatenate([_spread(got[:FREQ], 1), _spread(got[FREQ:], 0)], 1))
    du = _dot(jnp.concatenate(own, 0), mid_ref[...])
    both = _dot(jnp.concatenate(near, 0), side_ref[...])
    low = _low_lanes((2 * FREQ, 128))
    parts = []
    for p in range(2):
        d, n = du[:, p * TILE : p * TILE + TILE], both[:, p * 128 : p * 128 + 128]
        parts.append(
            jnp.concatenate(
                [d[:, :128] + jnp.where(low, n, 0.0), d[:, 128:384], d[:, 384:] + jnp.where(low, 0.0, n)], 1
            ).astype(BF)
        )
    copies = []
    for side in range(2):
        rows = pl.ds(side * AMBIT, AMBIT)
        stack = jnp.concatenate([p[side * FREQ : side * FREQ + FREQ] for p in parts], 0)
        staged[rows, :] = part_ref[rows, :] + _dot(far_ref[rows, :], stack)
        copy = pltpu.make_async_copy(
            staged.at[rows], out_ref.at[pl.ds(side * (2 * TILE - AMBIT), AMBIT)], sem.at[side]
        )
        copy.start()
        copies.append(copy)
    for copy in copies:
        copy.wait()


def _permute(value, target):
    bands, cols = lax.axis_size("own"), lax.axis_size("img")
    pairs = []
    for a in range(bands):
        for b in range(cols):
            c, d = target(a, b)
            pairs.append((a * cols + b, c * cols + d))
    return lax.ppermute(value, ("own", "img"), pairs)


def _img_even(a, b):
    return a, b ^ 1


def _img_odd(a, b):
    c = ((b + 1) ^ 1) - 1
    return (a, c) if 0 <= c < 32 else (a ^ 1, b)


def _own_even(a, b):
    return a ^ 1, b


def _own_odd(a, b):
    c = ((a + 1) ^ 1) - 1
    return (c, b) if 0 <= c < 4 else (a, b ^ 1)


def on_device(mask_field, target_field, occupancy, kernels, weights):
    t = {name: jnp.asarray(value) for name, value in TABLES.items()}
    vmem = pl.BlockSpec(memory_space=pltpu.VMEM)
    small = jax.ShapeDtypeStruct((FREQ, 128), F32)
    limit = lambda mib: pltpu.CompilerParams(vmem_limit_bytes=mib << 20)

    hbm = pl.BlockSpec(memory_space=pltpu.MemorySpace.HBM)
    even = lax.rem(lax.axis_index("own"), 2) == 0
    top, bottom = mask_field[:AMBIT], mask_field[2 * TILE - AMBIT :]
    ambit_a = jnp.where(even, bottom, top)
    ambit_b = jnp.where(even, top, bottom)
    halo_a = _permute(ambit_a, _own_even)
    halo_b = _permute(ambit_b, _own_odd)

    smem = pl.BlockSpec(memory_space=pltpu.SMEM)
    wide = jnp.sqrt(weights)[:, None, None] * kernels
    kk = jnp.concatenate([wide[0], wide[0], wide[1], wide[1]], -1)

    own, send_a, send_b = pl.pallas_call(
        _forward_kernel,
        out_shape=[small] * 3,
        in_specs=[vmem] * 8,
        out_specs=[vmem] * 3,
        scratch_shapes=[pltpu.VMEM((128, 512), BF)],
        compiler_params=limit(8),
        name="forward",
    )(mask_field, halo_a, halo_b, t["fwd"], t["fwd_ambit"], t["f_mid"], t["f_left"], t["f_right"])

    got_a = _permute(send_a, _img_even)
    got_b = _permute(send_b, _img_odd)

    grads = pl.pallas_call(
        _image_kernel,
        out_shape=small,
        in_specs=[vmem] * 5 + [smem] + [vmem] * 8,
        out_specs=vmem,
        scratch_shapes=[
            pltpu.VMEM((2, KERNELS, FREQ, 256), BF),
            pltpu.VMEM((KERNELS, GRID, 256), F32),
            pltpu.VMEM((2, KERNELS, FREQ, 256), BF),
            pltpu.VMEM((TILE, 128), BF),
        ],
        compiler_params=limit(24),
        name="image",
    )(
        own, got_a, got_b, kk, target_field, occupancy,
        t["tp"], t["te"], t["tx"], t["tv"], t["tz"], t["tw"], t["ty"], t["tg"],
    )

    side_a = _permute(grads, _img_even)
    side_b = _permute(grads, _img_odd)

    result = jax.ShapeDtypeStruct((2 * TILE, TILE), F32)
    middle, edges, rims = pl.pallas_call(
        _inner_kernel,
        out_shape=[result, jax.ShapeDtypeStruct((2 * TILE, 256), F32), jax.ShapeDtypeStruct((2 * AMBIT, 256), F32)],
        in_specs=[vmem] * 4,
        out_specs=[hbm, vmem, vmem],
        scratch_shapes=[
            pltpu.VMEM((128, TILE), BF),
            pltpu.VMEM((2 * TILE, 256), F32),
            pltpu.SemaphoreType.DMA((4,)),
        ],
        compiler_params=limit(8),
        name="inner",
    )(grads, mask_field, t["bwd"], t["b_mid"])

    pair = jax.ShapeDtypeStruct((2 * FREQ, 128), F32)
    send_a, send_b = pl.pallas_call(
        _glue_kernel,
        out_shape=[pair] * 2,
        in_specs=[vmem] * 4,
        out_specs=[vmem] * 2,
        compiler_params=limit(2),
        name="glue",
    )(rims, grads, side_a, side_b)
    tile_a = _permute(send_a, _own_even)
    tile_b = _permute(send_b, _own_odd)

    most, part = pl.pallas_call(
        _sides_kernel,
        out_shape=[result, jax.ShapeDtypeStruct((2 * AMBIT, TILE), F32)],
        in_specs=[hbm] + [vmem] * 6,
        out_specs=[hbm, vmem],
        scratch_shapes=[
            pltpu.VMEM((128, 128), BF),
            pltpu.VMEM((2 * TILE, 256), F32),
            pltpu.SemaphoreType.DMA((8,)),
        ],
        input_output_aliases={0: 0},
        compiler_params=limit(8),
        name="sides",
    )(middle, edges, rims, side_a, side_b, t["bwd"], t["b_side"])
    return pl.pallas_call(
        _rims_kernel,
        out_shape=result,
        in_specs=[hbm] + [vmem] * 6,
        out_specs=hbm,
        scratch_shapes=[pltpu.VMEM((2 * AMBIT, TILE), F32), pltpu.SemaphoreType.DMA((2,))],
        input_output_aliases={0: 0},
        compiler_params=limit(4),
        name="rims",
    )(most, part, tile_a, tile_b, t["far"], t["b_mid"], t["b_side"])


def solution(mesh):
    return jax.shard_map(
        on_device,
        mesh=mesh,
        in_specs=(P("own", "img"), P("own", "img"), P(), P(), P()),
        out_specs=P("own", "img"),
        check_vma=False,
    )
```

time: 31.5 us -> 28.2 us (0.90)
  waiting for transfers between devices: 9.08 us -> 5.64 us
  starting transfers between devices: 7.23 us -> 10.2 us
  Pallas kernels: 11.2 us -> 8.4 us
    ppermute x8, waiting for transfers between devices: 9.08 us -> 5.64 us  [_permute(): return lax.ppermute(value, ('own', 'img'), pairs)]
    ppermute x8, starting transfers between devices: 7.23 us -> 10.2 us  [_permute(): return lax.ppermute(value, ('own', 'img'), pairs)]
    pallas_call x4 -> x5, Pallas kernels: 10.7 us -> 7.88 us  [the longest x1 3.88 us: on_device(): pl.pallas_call(_image_kernel, out_shape=small, in_specs=[vmem] * 5 + [sme...]
  transfers between devices with their start and end apart: 8 -> 8, of which waited for: 6 -> 6; matrix products, arithmetic and copies ran while one was open for 7% -> 8% of each run, Pallas kernels for 7% -> 10%
where the time goes in v2:
time: 28.2 us; the launch traced here: 28 us
  starting transfers between devices  10.2 us (36%)
  Pallas kernels  8.4 us (30%)
  waiting for transfers between devices  5.64 us (20%)
  other arithmetic  2.63 us (9%)
  local copies, waits for them, and re-layouts  0.84 us (3%)
  between operations  0.32 us (1%)
    ppermute x8, starting transfers between devices, _permute(): return lax.ppermute(value, ('own', 'img'), pairs)  10.2 us
    ppermute x8, waiting for transfers between devices, _permute(): return lax.ppermute(value, ('own', 'img'), pairs)  5.64 us
    pallas_call x1, Pallas kernels, on_device(): pl.pallas_call(_image_kernel, out_shape=small, in_specs=[vmem] * 5 + [sme...  3.88 us
    pallas_call x1, Pallas kernels, on_device(): pl.pallas_call(_inner_kernel, out_shape=[result, jax.ShapeDtypeStruct((2...  1.39 us
    pallas_call x1, Pallas kernels, on_device(): pl.pallas_call(_sides_kernel, out_shape=[result, jax.ShapeDtypeStruct((2...  1.38 us
    mul x1, other arithmetic, on_device(): wide = jnp.sqrt(weights)[:, None, None] * kernels  1.25 us
    pallas_call x1, Pallas kernels, on_device(): pl.pallas_call(_rims_kernel, out_shape=result, in_specs=[hbm] + [vmem] *...  1.16 us
    select_n x1, other arithmetic, on_device(): ambit_b = jnp.where(even, top, bottom)  1.01 us
  transfers between devices with their start and end apart: 8, of which 6 were waited for; matrix products, arithmetic and copies ran while one was open for 8% of the time, Pallas kernels for 10%

profile of v2, /device:TPU:36, one launch (start us, length us, event | category | flops | bytes accessed | tf_op | source)
XLA Modules:
  0.0 28.0 jit_solution(3917937483138879815)
XLA Ops:
  0.0 0.0 copy-start.16
  0.1 1.0 %broadcast_select_fusion = (bf16[64,512]{1,0:T(8,128)(2,1)S(1)}, bf16[64,512]{1,0:T(8,128)(2,1)S(1)}) fusion(pred[]{:T(512)S(6)} %eq.3, bf16[1024,512]{1,0:T(8,128)(2,1)} %mask_ref.3), kind=kLoop, calls=%fused_computation.4 | loop fusion | flops 65536 | bytes 262145 | tf_op jit(solution)/shard_map/jit(_where)/select_n | solution.py:402
  1.1 2.0 %collective-permute-start.1 = (bf16[64,512]{1,0:T(8,128)(2,1)S(1)}, bf16[64,512]{1,0:T(8,128)(2,1)S(1)}, u32[]{:S(2)}, u32[]{:S(2)}) collective-permute-start(bf16[64,512]{1,0:T(8,128)(2,1)S(1)} %get-tuple-element.25), channel_id=1, source_target_pairs={{0,1},{1,0},{2,3},{3,2},{4,5},{5,4},{6,7},{7,6},{8,9},{9,8},{10,11... | collective-permute-start | bytes 196616 | tf_op jit(solution)/shard_map/ppermute | solution.py:371
  3.1 0.7 %sqrt.3 = f32[24]{0:T(128)S(1)} sqrt(f32[24]{0:T(128)} %param.26) | non-fusion elementwise | bytes 192 | tf_op jit(solution)/shard_map/sqrt | solution.py:407
  3.7 1.3 %broadcast_multiply_fusion = f32[2,24,32,32]{3,2,1,0:T(8,128)S(1)} fusion(f32[2,24,32,32]{3,2,1,0:T(8,128)} %param.25, f32[24]{0:T(128)S(1)} %sqrt.3), kind=kLoop, calls=%fused_computation.3 | loop fusion | flops 49152 | bytes 393312 | tf_op jit(solution)/shard_map/mul | solution.py:407
  5.1 0.1 slice_bitcast_fusion.1
  5.2 0.2 collective-permute-done.1.hb_ref
  5.4 1.9 %collective-permute-done.ha_ref = bf16[64,512]{1,0:T(8,128)(2,1)S(1)} collective-permute-done((bf16[64,512]{1,0:T(8,128)(2,1)S(1)}, bf16[64,512]{1,0:T(8,128)(2,1)S(1)}, u32[]{:S(2)}, u32[]{:S(2)}) %collective-permute-start) | collective-permute-done | bytes 65568 | tf_op jit(solution)/shard_map/ppermute | solution.py:371
  7.4 0.5 %forward.1 = (f32[32,128]{1,0:T(8,128)S(1)}, f32[32,128]{1,0:T(8,128)S(1)}, f32[32,128]{1,0:T(8,128)S(1)}) custom-call(bf16[1024,512]{1,0:T(8,128)(2,1)S(1)} %copy-done, bf16[64,512]{1,0:T(8,128)(2,1)S(1)} %collective-permute-done.ha_ref, bf16[64,512]{1,0:T(8,128)(2,1)S(1)} %collective-permute-done.1.hb_ref, bf16[128,1024]{1,0:T(8,128)(2,1)S(1)} %copy-done.7, ...), custom_call_target="tpu_custom_call" | custom-call | tf_op jit(solution)/shard_map/forward/pallas_call | solution.py:410
  7.9 0.1 collective-permute-start.2
  8.0 3.1 %collective-permute-start.3 = (f32[32,128]{1,0:T(8,128)S(1)}, f32[32,128]{1,0:T(8,128)S(1)}, u32[]{:S(2)}, u32[]{:S(2)}) collective-permute-start(f32[32,128]{1,0:T(8,128)S(1)} %get-tuple-element.17), channel_id=1, source_target_pairs={{0,32},{1,2},{2,1},{3,4},{4,3},{5,6},{6,5},{7,8},{8,7},{9,10},{10,... | collective-permute-start | bytes 49160 | tf_op jit(solution)/shard_map/ppermute | solution.py:371
  11.1 0.4 %pad_maximum_fusion.kk_ref = f32[24,32,128]{2,1,0:T(8,128)S(1)} fusion(f32[24,32,32]{2,1,0:T(8,128)S(1)} %get-tuple-element.28, f32[24,32,32]{2,1,0:T(8,128)S(1)} %get-tuple-element.27), kind=kLoop, calls=%fused_computation.2 | loop fusion | flops 294912 | bytes 589824 | tf_op jit(solution)/shard_map/concatenate | solution.py:408
  11.5 1.9 %collective-permute-done.3.xb_ref = f32[32,128]{1,0:T(8,128)S(1)} collective-permute-done((f32[32,128]{1,0:T(8,128)S(1)}, f32[32,128]{1,0:T(8,128)S(1)}, u32[]{:S(2)}, u32[]{:S(2)}) %collective-permute-start.3) | collective-permute-done | bytes 16416 | tf_op jit(solution)/shard_map/ppermute | solution.py:371
  13.5 3.9 %image.1.g_ref = f32[32,128]{1,0:T(8,128)S(1)} custom-call(f32[32,128]{1,0:T(8,128)S(1)} %get-tuple-element.15.x_ref, f32[32,128]{1,0:T(8,128)S(1)} %collective-permute-done.2.xa_ref, f32[32,128]{1,0:T(8,128)S(1)} %collective-permute-done.3.xb_ref, f32[24,32,128]{2,1,0:T(8,128)S(1)} %pad_maximum_fusion.kk_ref, bf16[1024,512]{1,0:T(8,128)(2,1)S(1)} %copy-done.3, ...), custom_call_target="tpu_custom_call" | custom-call | tf_op jit(solution)/shard_map/image/pallas_call | solution.py:423
  17.3 3.1 %collective-permute-start.5 = (f32[32,128]{1,0:T(8,128)S(1)}, f32[32,128]{1,0:T(8,128)S(1)}, u32[]{:S(2)}, u32[]{:S(2)}) collective-permute-start(f32[32,128]{1,0:T(8,128)S(1)} %image.1.g_ref), channel_id=1, source_target_pairs={{0,32},{1,2},{2,1},{3,4},{4,3},{5,6},{6,5},{7,8},{8,7},{9,10},{10,... | collective-permute-start | bytes 49160 | tf_op jit(solution)/shard_map/ppermute | solution.py:371
  20.4 1.4 %inner.1 = (f32[1024,512]{1,0:T(8,128)}, f32[1024,256]{1,0:T(8,128)S(1)}, f32[128,256]{1,0:T(8,128)S(1)}) custom-call(f32[32,128]{1,0:T(8,128)S(1)} %image.1.g_ref, bf16[1024,512]{1,0:T(8,128)(2,1)S(1)} %copy-done, bf16[1024,128]{1,0:T(8,128)(2,1)S(1)} %copy-done.1, bf16[128,1024]{1,0:T(8,128)(2,1)S(1)} %copy-done.2), custom_call_target="tpu_custom_call" | custom-call | tf_op jit(solution)/shard_map/inner/pallas_call | solution.py:445
  21.8 0.8 %collective-permute-done.5.sb_ref = f32[32,128]{1,0:T(8,128)S(1)} collective-permute-done((f32[32,128]{1,0:T(8,128)S(1)}, f32[32,128]{1,0:T(8,128)S(1)}, u32[]{:S(2)}, u32[]{:S(2)}) %collective-permute-start.5) | collective-permute-done | bytes 16416 | tf_op jit(solution)/shard_map/ppermute | solution.py:371
  22.7 0.1 glue.1
  22.8 0.1 collective-permute-start.6
  22.9 1.9 %collective-permute-start.7 = (f32[64,128]{1,0:T(8,128)S(1)}, f32[64,128]{1,0:T(8,128)S(1)}, u32[]{:S(2)}, u32[]{:S(2)}) collective-permute-start(f32[64,128]{1,0:T(8,128)S(1)} %get-tuple-element.24), channel_id=1, source_target_pairs={{0,1},{1,0},{2,3},{3,2},{4,5},{5,4},{6,7},{7,6},{8,9},{9,8},{10,11... | collective-permute-start | bytes 98312 | tf_op jit(solution)/shard_map/ppermute | solution.py:371
  24.7 1.4 %sides.1 = (f32[1024,512]{1,0:T(8,128)}, f32[128,512]{1,0:T(8,128)S(1)}) custom-call(f32[1024,512]{1,0:T(8,128)} %get-tuple-element.18.done_ref, f32[1024,256]{1,0:T(8,128)S(1)} %get-tuple-element.19.edge_ref, f32[128,256]{1,0:T(8,128)S(1)} %get-tuple-element.20.rim_ref.done_ref, ...), custom_call_target="tpu_custom_call", output_to_operand_aliasing={{0}: (0, {})} | custom-call | tf_op jit(solution)/shard_map/sides/pallas_call | solution.py:471
  26.1 0.7 %collective-permute-done.6.ta_ref = f32[64,128]{1,0:T(8,128)S(1)} collective-permute-done((f32[64,128]{1,0:T(8,128)S(1)}, f32[64,128]{1,0:T(8,128)S(1)}, u32[]{:S(2)}, u32[]{:S(2)}) %collective-permute-start.6) | collective-permute-done | bytes 32800 | tf_op jit(solution)/shard_map/ppermute | solution.py:371
  26.8 0.1 collective-permute-done.7.tb_ref
  26.8 1.2 %rims.1 = f32[1024,512]{1,0:T(8,128)} custom-call(f32[1024,512]{1,0:T(8,128)} %get-tuple-element.21.done_ref, f32[128,512]{1,0:T(8,128)S(1)} %get-tuple-element.22.part_ref, f32[64,128]{1,0:T(8,128)S(1)} %collective-permute-done.6.ta_ref, f32[64,128]{1,0:T(8,128)S(1)} %collective-permute-done.7.tb_ref, ...), custom_call_target="tpu_custom_call", output_to_operand_aliasing={{}: (0, {})} | custom-call | tf_op jit(solution)/shard_map/rims/pallas_call | solution.py:485
  (43 shorter events, 0.1 us)
Async XLA Ops:
  0.0 7.3 %copy-start.14 = (bf16[256,128]{1,0:T(8,128)(2,1)S(1)}, bf16[256,128]{1,0:T(8,128)(2,1)}, u32[]{:S(2)}) copy-start(bf16[256,128]{1,0:T(8,128)(2,1)} %constant.52.clone.left_ref) | copy-start | bytes 196612
  0.0 7.3 %copy-start.6 = (bf16[1024,128]{1,0:T(8,128)(2,1)S(1)}, bf16[1024,128]{1,0:T(8,128)(2,1)}, u32[]{:S(2)}) copy-start(bf16[1024,128]{1,0:T(8,128)(2,1)} %constant.50.clone.mid_ref) | copy-start | bytes 786436
  0.0 7.3 %copy-start.16 = (bf16[128,128]{1,0:T(8,128)(2,1)S(1)}, bf16[128,128]{1,0:T(8,128)(2,1)}, u32[]{:S(2)}) copy-start(bf16[128,128]{1,0:T(8,128)(2,1)} %constant.47.clone.ambit_ref) | copy-start | bytes 98308
  1.1 4.3 %collective-permute-start.1 = (bf16[64,512]{1,0:T(8,128)(2,1)S(1)}, bf16[64,512]{1,0:T(8,128)(2,1)S(1)}, u32[]{:S(2)}, u32[]{:S(2)}) collective-permute-start(bf16[64,512]{1,0:T(8,128)(2,1)S(1)} %get-tuple-element.25), channel_id=1, source_target_pairs={{0,1},{1,0},{2,3},{3,2},{4,5},{5,4},{6,7},{7,6},{8,9},{9,8},{10,11... | collective-permute-start | bytes 196616 | tf_op jit(solution)/shard_map/ppermute | solution.py:371
  3.1 4.3 %collective-permute-start = (bf16[64,512]{1,0:T(8,128)(2,1)S(1)}, bf16[64,512]{1,0:T(8,128)(2,1)S(1)}, u32[]{:S(2)}, u32[]{:S(2)}) collective-permute-start(bf16[64,512]{1,0:T(8,128)(2,1)S(1)} %get-tuple-element.26), channel_id=1, source_target_pairs={{0,32},{1,33},{2,34},{3,35},{4,36},{5,37},{6,38},{7,39},{8,40},{9,... | collective-permute-start | bytes 196616 | tf_op jit(solution)/shard_map/ppermute | solution.py:371
  5.0 8.4 %copy-start.3 = (bf16[1024,512]{1,0:T(8,128)(2,1)S(1)}, bf16[1024,512]{1,0:T(8,128)(2,1)}, u32[]{:S(2)}) copy-start(bf16[1024,512]{1,0:T(8,128)(2,1)} %target_ref.1) | copy-start | bytes 3145732
  5.0 8.4 %copy-start.5 = (bf16[384,512]{1,0:T(8,128)(2,1)S(1)}, bf16[384,512]{1,0:T(8,128)(2,1)}, u32[]{:S(2)}) copy-start(bf16[384,512]{1,0:T(8,128)(2,1)} %constant.59.clone.tz_ref) | copy-start | bytes 1179652
  5.0 8.4 %copy-start.8 = (bf16[512,256]{1,0:T(8,128)(2,1)S(1)}, bf16[512,256]{1,0:T(8,128)(2,1)}, u32[]{:S(2)}) copy-start(bf16[512,256]{1,0:T(8,128)(2,1)} %constant.61.clone.ty_ref) | copy-start | bytes 786436
  5.0 8.4 %copy-start.9 = (bf16[512,208]{1,0:T(8,128)(2,1)S(1)}, bf16[512,208]{1,0:T(8,128)(2,1)}, u32[]{:S(2)}) copy-start(bf16[512,208]{1,0:T(8,128)(2,1)} %constant.60.clone.tw_ref) | copy-start | bytes 638980
  5.0 8.4 %copy-start.10 = (bf16[128,512]{1,0:T(8,128)(2,1)S(1)}, bf16[128,512]{1,0:T(8,128)(2,1)}, u32[]{:S(2)}) copy-start(bf16[128,512]{1,0:T(8,128)(2,1)} %constant.62.clone.tg_ref) | copy-start | bytes 393220
  5.0 8.4 %copy-start.11 = (bf16[256,256]{1,0:T(8,128)(2,1)S(1)}, bf16[256,256]{1,0:T(8,128)(2,1)}, u32[]{:S(2)}) copy-start(bf16[256,256]{1,0:T(8,128)(2,1)} %constant.55.clone.tp_ref) | copy-start | bytes 393220
  5.1 8.3 %copy-start.12 = (bf16[256,128]{1,0:T(8,128)(2,1)S(1)}, bf16[256,128]{1,0:T(8,128)(2,1)}, u32[]{:S(2)}) copy-start(bf16[256,128]{1,0:T(8,128)(2,1)} %constant.58.clone.tv_ref) | copy-start | bytes 196612
  5.1 8.3 %copy-start.17 = (bf16[64,64]{1,0:T(8,128)(2,1)S(1)}, bf16[64,64]{1,0:T(8,128)(2,1)}, u32[]{:S(2)}) copy-start(bf16[64,64]{1,0:T(8,128)(2,1)} %constant.57.clone.tx_ref) | copy-start | bytes 24580
  5.1 8.3 %copy-start.18 = (bf16[64,128]{1,0:T(8,128)(2,1)S(1)}, bf16[64,128]{1,0:T(8,128)(2,1)}, u32[]{:S(2)}) copy-start(bf16[64,128]{1,0:T(8,128)(2,1)} %constant.56.clone.te_ref) | copy-start | bytes 49156
  5.1 8.3 %copy-start.19 = (s32[8,32]{1,0:T(8,128)S(1)}, s32[8,32]{1,0:T(8,128)}, u32[]{:S(2)}) copy-start(s32[8,32]{1,0:T(8,128)} %occ_ref.1) | copy-start | bytes 3076
  7.9 12.5 %copy-start.1 = (bf16[1024,128]{1,0:T(8,128)(2,1)S(1)}, bf16[1024,128]{1,0:T(8,128)(2,1)}, u32[]{:S(2)}) copy-start(bf16[1024,128]{1,0:T(8,128)(2,1)} %constant.48.clone.bwd_ref) | copy-start | bytes 786436
  7.9 12.5 %copy-start.2 = (bf16[128,1024]{1,0:T(8,128)(2,1)S(1)}, bf16[128,1024]{1,0:T(8,128)(2,1)}, u32[]{:S(2)}) copy-start(bf16[128,1024]{1,0:T(8,128)(2,1)} %constant.51.clone.mid_ref) | copy-start | bytes 786436
  7.9 3.6 %collective-permute-start.2 = (f32[32,128]{1,0:T(8,128)S(1)}, f32[32,128]{1,0:T(8,128)S(1)}, u32[]{:S(2)}, u32[]{:S(2)}) collective-permute-start(f32[32,128]{1,0:T(8,128)S(1)} %get-tuple-element.16), channel_id=1, source_target_pairs={{0,1},{1,0},{2,3},{3,2},{4,5},{5,4},{6,7},{7,6},{8,9},{9,8},{10,11... | collective-permute-start | bytes 49160 | tf_op jit(solution)/shard_map/ppermute | solution.py:371
  8.0 5.4 %collective-permute-start.3 = (f32[32,128]{1,0:T(8,128)S(1)}, f32[32,128]{1,0:T(8,128)S(1)}, u32[]{:S(2)}, u32[]{:S(2)}) collective-permute-start(f32[32,128]{1,0:T(8,128)S(1)} %get-tuple-element.17), channel_id=1, source_target_pairs={{0,32},{1,2},{2,1},{3,4},{4,3},{5,6},{6,5},{7,8},{8,7},{9,10},{10,... | collective-permute-start | bytes 49160 | tf_op jit(solution)/shard_map/ppermute | solution.py:371
  13.4 11.3 %copy-start.4 = (bf16[256,256]{1,0:T(8,128)(2,1)S(1)}, bf16[256,256]{1,0:T(8,128)(2,1)}, u32[]{:S(2)}) copy-start(bf16[256,256]{1,0:T(8,128)(2,1)} %constant.54.clone.side_ref) | copy-start | bytes 393220
  17.3 5.3 %collective-permute-start.5 = (f32[32,128]{1,0:T(8,128)S(1)}, f32[32,128]{1,0:T(8,128)S(1)}, u32[]{:S(2)}, u32[]{:S(2)}) collective-permute-start(f32[32,128]{1,0:T(8,128)S(1)} %image.1.g_ref), channel_id=1, source_target_pairs={{0,32},{1,2},{2,1},{3,4},{4,3},{5,6},{6,5},{7,8},{8,7},{9,10},{10,... | collective-permute-start | bytes 49160 | tf_op jit(solution)/shard_map/ppermute | solution.py:371
  20.4 2.3 %collective-permute-start.4 = (f32[32,128]{1,0:T(8,128)S(1)}, f32[32,128]{1,0:T(8,128)S(1)}, u32[]{:S(2)}, u32[]{:S(2)}) collective-permute-start(f32[32,128]{1,0:T(8,128)S(1)} %image.1.g_ref), channel_id=1, source_target_pairs={{0,1},{1,0},{2,3},{3,2},{4,5},{5,4},{6,7},{7,6},{8,9},{9,8},{10,11... | collective-permute-start | bytes 49160 | tf_op jit(solution)/shard_map/ppermute | solution.py:371
  22.8 4.0 %collective-permute-start.6 = (f32[64,128]{1,0:T(8,128)S(1)}, f32[64,128]{1,0:T(8,128)S(1)}, u32[]{:S(2)}, u32[]{:S(2)}) collective-permute-start(f32[64,128]{1,0:T(8,128)S(1)} %get-tuple-element.23), channel_id=1, source_target_pairs={{0,32},{1,33},{2,34},{3,35},{4,36},{5,37},{6,38},{7,39},{8,40},{9,... | collective-permute-start | bytes 98312 | tf_op jit(solution)/shard_map/ppermute | solution.py:371
  22.9 4.0 %collective-permute-start.7 = (f32[64,128]{1,0:T(8,128)S(1)}, f32[64,128]{1,0:T(8,128)S(1)}, u32[]{:S(2)}, u32[]{:S(2)}) collective-permute-start(f32[64,128]{1,0:T(8,128)S(1)} %get-tuple-element.24), channel_id=1, source_target_pairs={{0,1},{1,0},{2,3},{3,2},{4,5},{5,4},{6,7},{7,6},{8,9},{9,8},{10,11... | collective-permute-start | bytes 98312 | tf_op jit(solution)/shard_map/ppermute | solution.py:371
  (4 other events, 27.0 us)

commit v3 on v2

--- a/solution.py
+++ b/solution.py
@@ -5,6 +5,7 @@
 from jax.experimental import pallas as pl
 from jax.experimental.pallas import tpu as pltpu
 from jax.sharding import PartitionSpec as P
+
 
 TILE = 512
 AMBIT = 64
@@ -191,6 +192,7 @@
                 ],
                 0,
             )
+
         hi = halves(p_hi)
         e = _dot(te_ref[...], jnp.concatenate([hi, hi], 0))
         fields[k] = e
@@ -239,8 +241,8 @@
     turn = lambda x: pltpu.roll(x, 64, 1)
     first = jnp.concatenate([jnp.where(low, own, turn(left)), jnp.where(low, right, 0.0)], 0)
     second = jnp.concatenate([jnp.where(low, turn(own), left), jnp.where(low, turn(right), 0.0)], 0)
-    ta_ref[...] = jnp.where(even, second, first)
-    tb_ref[...] = jnp.where(even, first, second)
+    ta_ref[...] = jnp.where(even, second, first).astype(BF)
+    tb_ref[...] = jnp.where(even, first, second).astype(BF)
 
 
 def _by_side(sa_ref, sb_ref):
@@ -330,8 +332,8 @@
 def _rims_kernel(done_ref, part_ref, ta_ref, tb_ref, far_ref, mid_ref, side_ref, out_ref, staged, sem):
     band = lax.axis_index("own")
     even = lax.rem(band, 2) == 0
-    ta = ta_ref[...]
-    tb = jnp.where((band == 1) | (band == 2), tb_ref[...], 0.0)
+    ta = ta_ref[...].astype(F32)
+    tb = jnp.where((band == 1) | (band == 2), tb_ref[...].astype(F32), 0.0)
     own, near = [], []
     for got in (jnp.where(even, tb, ta), jnp.where(even, ta, tb)):
         own.append(_spread(got[:FREQ], 0))
@@ -361,7 +363,7 @@
         copy.wait()
 
 
-def _permute(value, target):
+def _exchange(value, target):
     bands, cols = lax.axis_size("own"), lax.axis_size("img")
     pairs = []
     for a in range(bands):
@@ -400,8 +402,8 @@
     top, bottom = mask_field[:AMBIT], mask_field[2 * TILE - AMBIT :]
     ambit_a = jnp.where(even, bottom, top)
     ambit_b = jnp.where(even, top, bottom)
-    halo_a = _permute(ambit_a, _own_even)
-    halo_b = _permute(ambit_b, _own_odd)
+    halo_a = _exchange(ambit_a, _own_even)
+    halo_b = _exchange(ambit_b, _own_odd)
 
     smem = pl.BlockSpec(memory_space=pltpu.SMEM)
     wide = jnp.sqrt(weights)[:, None, None] * kernels
@@ -417,8 +419,8 @@
         name="forward",
     )(mask_field, halo_a, halo_b, t["fwd"], t["fwd_ambit"], t["f_mid"], t["f_left"], t["f_right"])
 
-    got_a = _permute(send_a, _img_even)
-    got_b = _permute(send_b, _img_odd)
+    got_a = _exchange(send_a, _img_even)
+    got_b = _exchange(send_b, _img_odd)
 
     grads = pl.pallas_call(
         _image_kernel,
@@ -438,8 +440,8 @@
         t["tp"], t["te"], t["tx"], t["tv"], t["tz"], t["tw"], t["ty"], t["tg"],
     )
 
-    side_a = _permute(grads, _img_even)
-    side_b = _permute(grads, _img_odd)
+    side_a = _exchange(grads, _img_even)
+    side_b = _exchange(grads, _img_odd)
 
     result = jax.ShapeDtypeStruct((2 * TILE, TILE), F32)
     middle, edges, rims = pl.pallas_call(
@@ -456,7 +458,7 @@
         name="inner",
     )(grads, mask_field, t["bwd"], t["b_mid"])
 
-    pair = jax.ShapeDtypeStruct((2 * FREQ, 128), F32)
+    pair = jax.ShapeDtypeStruct((2 * FREQ, 128), BF)
     send_a, send_b = pl.pallas_call(
         _glue_kernel,
         out_shape=[pair] * 2,
@@ -465,8 +467,8 @@
         compiler_params=limit(2),
         name="glue",
     )(rims, grads, side_a, side_b)
-    tile_a = _permute(send_a, _own_even)
-    tile_b = _permute(send_b, _own_odd)
+    tile_a = _exchange(send_a, _own_even)
+    tile_b = _exchange(send_b, _own_odd)
 
     most, part = pl.pallas_call(
         _sides_kernel,

time: 28.2 us -> 28.2 us (level)
  no operation moved by 1% of the time
where the time goes in v3:
time: 28.2 us; the launch traced here: 27.8 us
  starting transfers between devices  10.2 us (36%)
  Pallas kernels  8.41 us (30%)
  waiting for transfers between devices  5.47 us (19%)
  other arithmetic  2.63 us (9%)
  local copies, waits for them, and re-layouts  0.84 us (3%)
  between operations  0.32 us (1%)
    ppermute x8, starting transfers between devices, _exchange(): return lax.ppermute(value, ('own', 'img'), pairs)  10.2 us
    ppermute x8, waiting for transfers between devices, _exchange(): return lax.ppermute(value, ('own', 'img'), pairs)  5.47 us
    pallas_call x1, Pallas kernels, on_device(): pl.pallas_call(_image_kernel, out_shape=small, in_specs=[vmem] * 5 + [sme...  3.88 us
    pallas_call x1, Pallas kernels, on_device(): pl.pallas_call(_inner_kernel, out_shape=[result, jax.ShapeDtypeStruct((2...  1.39 us
    pallas_call x1, Pallas kernels, on_device(): pl.pallas_call(_sides_kernel, out_shape=[result, jax.ShapeDtypeStruct((2...  1.38 us
    mul x1, other arithmetic, on_device(): wide = jnp.sqrt(weights)[:, None, None] * kernels  1.25 us
    pallas_call x1, Pallas kernels, on_device(): pl.pallas_call(_rims_kernel, out_shape=result, in_specs=[hbm] + [vmem] *...  1.16 us
    select_n x1, other arithmetic, on_device(): ambit_b = jnp.where(even, top, bottom)  1.01 us
  transfers between devices with their start and end apart: 8, of which 6 were waited for; matrix products, arithmetic and copies ran while one was open for 8% of the time, Pallas kernels for 10%

profile of v3, /device:TPU:36, one launch (start us, length us, event | category | flops | bytes accessed | tf_op | source)
XLA Modules:
  0.0 27.8 jit_solution(17057570491309048856)
XLA Ops:
  0.0 0.0 copy-start.16
  0.1 1.0 %broadcast_select_fusion = (bf16[64,512]{1,0:T(8,128)(2,1)S(1)}, bf16[64,512]{1,0:T(8,128)(2,1)S(1)}) fusion(pred[]{:T(512)S(6)} %eq.3, bf16[1024,512]{1,0:T(8,128)(2,1)} %mask_ref.3), kind=kLoop, calls=%fused_computation.4 | loop fusion | flops 65536 | bytes 262145 | tf_op jit(solution)/shard_map/jit(_where)/select_n | solution.py:404
  1.1 2.0 %collective-permute-start.1 = (bf16[64,512]{1,0:T(8,128)(2,1)S(1)}, bf16[64,512]{1,0:T(8,128)(2,1)S(1)}, u32[]{:S(2)}, u32[]{:S(2)}) collective-permute-start(bf16[64,512]{1,0:T(8,128)(2,1)S(1)} %get-tuple-element.25), channel_id=1, source_target_pairs={{0,1},{1,0},{2,3},{3,2},{4,5},{5,4},{6,7},{7,6},{8,9},{9,8},{10,11... | collective-permute-start | bytes 196616 | tf_op jit(solution)/shard_map/ppermute | solution.py:373
  3.1 0.7 %sqrt.3 = f32[24]{0:T(128)S(1)} sqrt(f32[24]{0:T(128)} %param.26) | non-fusion elementwise | bytes 192 | tf_op jit(solution)/shard_map/sqrt | solution.py:409
  3.7 1.3 %broadcast_multiply_fusion = f32[2,24,32,32]{3,2,1,0:T(8,128)S(1)} fusion(f32[2,24,32,32]{3,2,1,0:T(8,128)} %param.25, f32[24]{0:T(128)S(1)} %sqrt.3), kind=kLoop, calls=%fused_computation.3 | loop fusion | flops 49152 | bytes 393312 | tf_op jit(solution)/shard_map/mul | solution.py:409
  5.1 0.1 slice_bitcast_fusion.1
  5.2 0.2 collective-permute-done.1.hb_ref
  5.4 1.9 %collective-permute-done.ha_ref = bf16[64,512]{1,0:T(8,128)(2,1)S(1)} collective-permute-done((bf16[64,512]{1,0:T(8,128)(2,1)S(1)}, bf16[64,512]{1,0:T(8,128)(2,1)S(1)}, u32[]{:S(2)}, u32[]{:S(2)}) %collective-permute-start) | collective-permute-done | bytes 65568 | tf_op jit(solution)/shard_map/ppermute | solution.py:373
  7.4 0.5 %forward.1 = (f32[32,128]{1,0:T(8,128)S(1)}, f32[32,128]{1,0:T(8,128)S(1)}, f32[32,128]{1,0:T(8,128)S(1)}) custom-call(bf16[1024,512]{1,0:T(8,128)(2,1)S(1)} %copy-done, bf16[64,512]{1,0:T(8,128)(2,1)S(1)} %collective-permute-done.ha_ref, bf16[64,512]{1,0:T(8,128)(2,1)S(1)} %collective-permute-done.1.hb_ref, bf16[128,1024]{1,0:T(8,128)(2,1)S(1)} %copy-done.7, ...), custom_call_target="tpu_custom_call" | custom-call | tf_op jit(solution)/shard_map/forward/pallas_call | solution.py:412
  7.9 0.1 collective-permute-start.2
  8.0 3.1 %collective-permute-start.3 = (f32[32,128]{1,0:T(8,128)S(1)}, f32[32,128]{1,0:T(8,128)S(1)}, u32[]{:S(2)}, u32[]{:S(2)}) collective-permute-start(f32[32,128]{1,0:T(8,128)S(1)} %get-tuple-element.17), channel_id=1, source_target_pairs={{0,32},{1,2},{2,1},{3,4},{4,3},{5,6},{6,5},{7,8},{8,7},{9,10},{10,... | collective-permute-start | bytes 49160 | tf_op jit(solution)/shard_map/ppermute | solution.py:373
  11.1 0.4 %pad_maximum_fusion.kk_ref = f32[24,32,128]{2,1,0:T(8,128)S(1)} fusion(f32[24,32,32]{2,1,0:T(8,128)S(1)} %get-tuple-element.28, f32[24,32,32]{2,1,0:T(8,128)S(1)} %get-tuple-element.27), kind=kLoop, calls=%fused_computation.2 | loop fusion | flops 294912 | bytes 589824 | tf_op jit(solution)/shard_map/concatenate | solution.py:410
  11.5 1.9 %collective-permute-done.3.xb_ref = f32[32,128]{1,0:T(8,128)S(1)} collective-permute-done((f32[32,128]{1,0:T(8,128)S(1)}, f32[32,128]{1,0:T(8,128)S(1)}, u32[]{:S(2)}, u32[]{:S(2)}) %collective-permute-start.3) | collective-permute-done | bytes 16416 | tf_op jit(solution)/shard_map/ppermute | solution.py:373
  13.5 3.9 %image.1.g_ref = f32[32,128]{1,0:T(8,128)S(1)} custom-call(f32[32,128]{1,0:T(8,128)S(1)} %get-tuple-element.15.x_ref, f32[32,128]{1,0:T(8,128)S(1)} %collective-permute-done.2.xa_ref, f32[32,128]{1,0:T(8,128)S(1)} %collective-permute-done.3.xb_ref, f32[24,32,128]{2,1,0:T(8,128)S(1)} %pad_maximum_fusion.kk_ref, bf16[1024,512]{1,0:T(8,128)(2,1)S(1)} %copy-done.3, ...), custom_call_target="tpu_custom_call" | custom-call | tf_op jit(solution)/shard_map/image/pallas_call | solution.py:425
  17.3 3.1 %collective-permute-start.5 = (f32[32,128]{1,0:T(8,128)S(1)}, f32[32,128]{1,0:T(8,128)S(1)}, u32[]{:S(2)}, u32[]{:S(2)}) collective-permute-start(f32[32,128]{1,0:T(8,128)S(1)} %image.1.g_ref), channel_id=1, source_target_pairs={{0,32},{1,2},{2,1},{3,4},{4,3},{5,6},{6,5},{7,8},{8,7},{9,10},{10,... | collective-permute-start | bytes 49160 | tf_op jit(solution)/shard_map/ppermute | solution.py:373
  20.4 1.4 %inner.1 = (f32[1024,512]{1,0:T(8,128)}, f32[1024,256]{1,0:T(8,128)S(1)}, f32[128,256]{1,0:T(8,128)S(1)}) custom-call(f32[32,128]{1,0:T(8,128)S(1)} %image.1.g_ref, bf16[1024,512]{1,0:T(8,128)(2,1)S(1)} %copy-done, bf16[1024,128]{1,0:T(8,128)(2,1)S(1)} %copy-done.1, bf16[128,1024]{1,0:T(8,128)(2,1)S(1)} %copy-done.2), custom_call_target="tpu_custom_call" | custom-call | tf_op jit(solution)/shard_map/inner/pallas_call | solution.py:447
  21.8 0.8 %collective-permute-done.5.sb_ref = f32[32,128]{1,0:T(8,128)S(1)} collective-permute-done((f32[32,128]{1,0:T(8,128)S(1)}, f32[32,128]{1,0:T(8,128)S(1)}, u32[]{:S(2)}, u32[]{:S(2)}) %collective-permute-start.5) | collective-permute-done | bytes 16416 | tf_op jit(solution)/shard_map/ppermute | solution.py:373
  22.7 0.1 glue.1
  22.8 0.1 collective-permute-start.6
  22.9 1.9 %collective-permute-start.7 = (bf16[64,128]{1,0:T(8,128)(2,1)S(1)}, bf16[64,128]{1,0:T(8,128)(2,1)S(1)}, u32[]{:S(2)}, u32[]{:S(2)}) collective-permute-start(bf16[64,128]{1,0:T(8,128)(2,1)S(1)} %get-tuple-element.24), channel_id=1, source_target_pairs={{0,1},{1,0},{2,3},{3,2},{4,5},{5,4},{6,7},{7,6},{8,9},{9,8},{10,11... | collective-permute-start | bytes 49160 | tf_op jit(solution)/shard_map/ppermute | solution.py:373
  24.7 1.4 %sides.1 = (f32[1024,512]{1,0:T(8,128)}, f32[128,512]{1,0:T(8,128)S(1)}) custom-call(f32[1024,512]{1,0:T(8,128)} %get-tuple-element.18.done_ref, f32[1024,256]{1,0:T(8,128)S(1)} %get-tuple-element.19.edge_ref, f32[128,256]{1,0:T(8,128)S(1)} %get-tuple-element.20.rim_ref.done_ref, ...), custom_call_target="tpu_custom_call", output_to_operand_aliasing={{0}: (0, {})} | custom-call | tf_op jit(solution)/shard_map/sides/pallas_call | solution.py:473
  26.1 0.5 %collective-permute-done.6.ta_ref = bf16[64,128]{1,0:T(8,128)(2,1)S(1)} collective-permute-done((bf16[64,128]{1,0:T(8,128)(2,1)S(1)}, bf16[64,128]{1,0:T(8,128)(2,1)S(1)}, u32[]{:S(2)}, u32[]{:S(2)}) %collective-permute-start.6) | collective-permute-done | bytes 16416 | tf_op jit(solution)/shard_map/ppermute | solution.py:373
  26.6 0.1 collective-permute-done.7.tb_ref
  26.7 1.2 %rims.1 = f32[1024,512]{1,0:T(8,128)} custom-call(f32[1024,512]{1,0:T(8,128)} %get-tuple-element.21.done_ref, f32[128,512]{1,0:T(8,128)S(1)} %get-tuple-element.22.part_ref, bf16[64,128]{1,0:T(8,128)(2,1)S(1)} %collective-permute-done.6.ta_ref, bf16[64,128]{1,0:T(8,128)(2,1)S(1)} %collective-permute-done.7.tb_ref, ...), custom_call_target="tpu_custom_call", output_to_operand_aliasing={{}: (0, {})} | custom-call | tf_op jit(solution)/shard_map/rims/pallas_call | solution.py:487
  (43 shorter events, 0.1 us)
Async XLA Ops:
  0.0 7.3 %copy-start.14 = (bf16[256,128]{1,0:T(8,128)(2,1)S(1)}, bf16[256,128]{1,0:T(8,128)(2,1)}, u32[]{:S(2)}) copy-start(bf16[256,128]{1,0:T(8,128)(2,1)} %constant.52.clone.left_ref) | copy-start | bytes 196612
  0.0 7.3 %copy-start.6 = (bf16[1024,128]{1,0:T(8,128)(2,1)S(1)}, bf16[1024,128]{1,0:T(8,128)(2,1)}, u32[]{:S(2)}) copy-start(bf16[1024,128]{1,0:T(8,128)(2,1)} %constant.50.clone.mid_ref) | copy-start | bytes 786436
  0.0 7.3 %copy-start.16 = (bf16[128,128]{1,0:T(8,128)(2,1)S(1)}, bf16[128,128]{1,0:T(8,128)(2,1)}, u32[]{:S(2)}) copy-start(bf16[128,128]{1,0:T(8,128)(2,1)} %constant.47.clone.ambit_ref) | copy-start | bytes 98308
  1.1 4.3 %collective-permute-start.1 = (bf16[64,512]{1,0:T(8,128)(2,1)S(1)}, bf16[64,512]{1,0:T(8,128)(2,1)S(1)}, u32[]{:S(2)}, u32[]{:S(2)}) collective-permute-start(bf16[64,512]{1,0:T(8,128)(2,1)S(1)} %get-tuple-element.25), channel_id=1, source_target_pairs={{0,1},{1,0},{2,3},{3,2},{4,5},{5,4},{6,7},{7,6},{8,9},{9,8},{10,11... | collective-permute-start | bytes 196616 | tf_op jit(solution)/shard_map/ppermute | solution.py:373
  3.1 4.3 %collective-permute-start = (bf16[64,512]{1,0:T(8,128)(2,1)S(1)}, bf16[64,512]{1,0:T(8,128)(2,1)S(1)}, u32[]{:S(2)}, u32[]{:S(2)}) collective-permute-start(bf16[64,512]{1,0:T(8,128)(2,1)S(1)} %get-tuple-element.26), channel_id=1, source_target_pairs={{0,32},{1,33},{2,34},{3,35},{4,36},{5,37},{6,38},{7,39},{8,40},{9,... | collective-permute-start | bytes 196616 | tf_op jit(solution)/shard_map/ppermute | solution.py:373
  5.0 8.4 %copy-start.3 = (bf16[1024,512]{1,0:T(8,128)(2,1)S(1)}, bf16[1024,512]{1,0:T(8,128)(2,1)}, u32[]{:S(2)}) copy-start(bf16[1024,512]{1,0:T(8,128)(2,1)} %target_ref.1) | copy-start | bytes 3145732
  5.0 8.4 %copy-start.5 = (bf16[384,512]{1,0:T(8,128)(2,1)S(1)}, bf16[384,512]{1,0:T(8,128)(2,1)}, u32[]{:S(2)}) copy-start(bf16[384,512]{1,0:T(8,128)(2,1)} %constant.59.clone.tz_ref) | copy-start | bytes 1179652
  5.0 8.4 %copy-start.8 = (bf16[512,256]{1,0:T(8,128)(2,1)S(1)}, bf16[512,256]{1,0:T(8,128)(2,1)}, u32[]{:S(2)}) copy-start(bf16[512,256]{1,0:T(8,128)(2,1)} %constant.61.clone.ty_ref) | copy-start | bytes 786436
  5.0 8.4 %copy-start.9 = (bf16[512,208]{1,0:T(8,128)(2,1)S(1)}, bf16[512,208]{1,0:T(8,128)(2,1)}, u32[]{:S(2)}) copy-start(bf16[512,208]{1,0:T(8,128)(2,1)} %constant.60.clone.tw_ref) | copy-start | bytes 638980
  5.0 8.4 %copy-start.10 = (bf16[128,512]{1,0:T(8,128)(2,1)S(1)}, bf16[128,512]{1,0:T(8,128)(2,1)}, u32[]{:S(2)}) copy-start(bf16[128,512]{1,0:T(8,128)(2,1)} %constant.62.clone.tg_ref) | copy-start | bytes 393220
  5.0 8.4 %copy-start.11 = (bf16[256,256]{1,0:T(8,128)(2,1)S(1)}, bf16[256,256]{1,0:T(8,128)(2,1)}, u32[]{:S(2)}) copy-start(bf16[256,256]{1,0:T(8,128)(2,1)} %constant.55.clone.tp_ref) | copy-start | bytes 393220
  5.1 8.3 %copy-start.12 = (bf16[256,128]{1,0:T(8,128)(2,1)S(1)}, bf16[256,128]{1,0:T(8,128)(2,1)}, u32[]{:S(2)}) copy-start(bf16[256,128]{1,0:T(8,128)(2,1)} %constant.58.clone.tv_ref) | copy-start | bytes 196612
  5.1 8.3 %copy-start.17 = (bf16[64,64]{1,0:T(8,128)(2,1)S(1)}, bf16[64,64]{1,0:T(8,128)(2,1)}, u32[]{:S(2)}) copy-start(bf16[64,64]{1,0:T(8,128)(2,1)} %constant.57.clone.tx_ref) | copy-start | bytes 24580
  5.1 8.3 %copy-start.18 = (bf16[64,128]{1,0:T(8,128)(2,1)S(1)}, bf16[64,128]{1,0:T(8,128)(2,1)}, u32[]{:S(2)}) copy-start(bf16[64,128]{1,0:T(8,128)(2,1)} %constant.56.clone.te_ref) | copy-start | bytes 49156
  5.1 8.3 %copy-start.19 = (s32[8,32]{1,0:T(8,128)S(1)}, s32[8,32]{1,0:T(8,128)}, u32[]{:S(2)}) copy-start(s32[8,32]{1,0:T(8,128)} %occ_ref.1) | copy-start | bytes 3076
  7.9 12.5 %copy-start.1 = (bf16[1024,128]{1,0:T(8,128)(2,1)S(1)}, bf16[1024,128]{1,0:T(8,128)(2,1)}, u32[]{:S(2)}) copy-start(bf16[1024,128]{1,0:T(8,128)(2,1)} %constant.48.clone.bwd_ref) | copy-start | bytes 786436
  7.9 12.5 %copy-start.2 = (bf16[128,1024]{1,0:T(8,128)(2,1)S(1)}, bf16[128,1024]{1,0:T(8,128)(2,1)}, u32[]{:S(2)}) copy-start(bf16[128,1024]{1,0:T(8,128)(2,1)} %constant.51.clone.mid_ref) | copy-start | bytes 786436
  7.9 3.6 %collective-permute-start.2 = (f32[32,128]{1,0:T(8,128)S(1)}, f32[32,128]{1,0:T(8,128)S(1)}, u32[]{:S(2)}, u32[]{:S(2)}) collective-permute-start(f32[32,128]{1,0:T(8,128)S(1)} %get-tuple-element.16), channel_id=1, source_target_pairs={{0,1},{1,0},{2,3},{3,2},{4,5},{5,4},{6,7},{7,6},{8,9},{9,8},{10,11... | collective-permute-start | bytes 49160 | tf_op jit(solution)/shard_map/ppermute | solution.py:373
  8.0 5.4 %collective-permute-start.3 = (f32[32,128]{1,0:T(8,128)S(1)}, f32[32,128]{1,0:T(8,128)S(1)}, u32[]{:S(2)}, u32[]{:S(2)}) collective-permute-start(f32[32,128]{1,0:T(8,128)S(1)} %get-tuple-element.17), channel_id=1, source_target_pairs={{0,32},{1,2},{2,1},{3,4},{4,3},{5,6},{6,5},{7,8},{8,7},{9,10},{10,... | collective-permute-start | bytes 49160 | tf_op jit(solution)/shard_map/ppermute | solution.py:373
  13.4 11.3 %copy-start.4 = (bf16[256,256]{1,0:T(8,128)(2,1)S(1)}, bf16[256,256]{1,0:T(8,128)(2,1)}, u32[]{:S(2)}) copy-start(bf16[256,256]{1,0:T(8,128)(2,1)} %constant.54.clone.side_ref) | copy-start | bytes 393220
  17.3 5.3 %collective-permute-start.5 = (f32[32,128]{1,0:T(8,128)S(1)}, f32[32,128]{1,0:T(8,128)S(1)}, u32[]{:S(2)}, u32[]{:S(2)}) collective-permute-start(f32[32,128]{1,0:T(8,128)S(1)} %image.1.g_ref), channel_id=1, source_target_pairs={{0,32},{1,2},{2,1},{3,4},{4,3},{5,6},{6,5},{7,8},{8,7},{9,10},{10,... | collective-permute-start | bytes 49160 | tf_op jit(solution)/shard_map/ppermute | solution.py:373
  20.4 2.3 %collective-permute-start.4 = (f32[32,128]{1,0:T(8,128)S(1)}, f32[32,128]{1,0:T(8,128)S(1)}, u32[]{:S(2)}, u32[]{:S(2)}) collective-permute-start(f32[32,128]{1,0:T(8,128)S(1)} %image.1.g_ref), channel_id=1, source_target_pairs={{0,1},{1,0},{2,3},{3,2},{4,5},{5,4},{6,7},{7,6},{8,9},{9,8},{10,11... | collective-permute-start | bytes 49160 | tf_op jit(solution)/shard_map/ppermute | solution.py:373
  22.8 3.8 %collective-permute-start.6 = (bf16[64,128]{1,0:T(8,128)(2,1)S(1)}, bf16[64,128]{1,0:T(8,128)(2,1)S(1)}, u32[]{:S(2)}, u32[]{:S(2)}) collective-permute-start(bf16[64,128]{1,0:T(8,128)(2,1)S(1)} %get-tuple-element.23), channel_id=1, source_target_pairs={{0,32},{1,33},{2,34},{3,35},{4,36},{5,37},{6,38},{7,39},{8,40},{9,... | collective-permute-start | bytes 49160 | tf_op jit(solution)/shard_map/ppermute | solution.py:373
  22.9 3.8 %collective-permute-start.7 = (bf16[64,128]{1,0:T(8,128)(2,1)S(1)}, bf16[64,128]{1,0:T(8,128)(2,1)S(1)}, u32[]{:S(2)}, u32[]{:S(2)}) collective-permute-start(bf16[64,128]{1,0:T(8,128)(2,1)S(1)} %get-tuple-element.24), channel_id=1, source_target_pairs={{0,1},{1,0},{2,3},{3,2},{4,5},{5,4},{6,7},{7,6},{8,9},{9,8},{10,11... | collective-permute-start | bytes 49160 | tf_op jit(solution)/shard_map/ppermute | solution.py:373
  (4 other events, 26.8 us)
